TPU v7x, 256 devices: a whole 4x4x8 slice. The times are simulated.
256 devices in a mesh: cuts: 2 (over core), tile: 128 (over z, y, x).
Axes of the slice: x: 4, y: 4, z: 8, core: 2. Of those that a mesh axis runs over, the one named last changes fastest.
Arguments:
- transmission: float32 [2, 2, 32768, 512], P(None, 'cuts', 'tile')
- illumination: float32 [2, 256, 256], replicated, may hold values from -6 to 6
- measured: float32 [128, 256, 256], P('tile'), may hold values from 0.2 to 5
- offsets: int32 [128, 2], P('tile'), may hold values from 0 to 256, as said below
- live_count: int32 [128], P('tile'), may hold values from 1 to 1, as said below
Outputs:
- object_grad: float32 [2, 2, 32768, 512], P(None, 'cuts', 'tile')
Inputs may be any that keep to these rules, and one draw needn't show every extreme that they name: offsets[j, 0] counts rows from the first row of tile j // 1 and may run past that tile's end (past the last tile, into the first); offsets[j, 1] counts columns; in every draw some live slot has row 255 and column 256. `live_count`: slots of a tile at or beyond its count are unused; some tile has all 1 slots used in every draw.
All inputs are finite; a program needn't handle non-finite values.
Results may differ from a plain program's by a relative error of at most 0.0049.
Values may be sent and summed in bfloat16 or wider, within the bound.
No kernel may reach another device: no remote copies, remote signals or barrier semaphores. Data moves between devices by JAX's collectives and lax.ppermute only.
A program may use at most 64 MiB of HBM per device.

v0:
```python
import math

import jax
import jax.numpy as jnp
from jax import lax
from jax.sharding import PartitionSpec as P


def shifted(value, axis, steps):
    count = lax.axis_size(axis)
    pairs = [(source, (source + steps) % count) for source in range(count)]
    return lax.ppermute(value, axis, pairs)


def passed_along(value, axis, steps):
    count = lax.axis_size(axis)
    first, last = (max(0, -steps), min(count, count - steps))
    return lax.ppermute(value, axis, [(source, source + steps) for source in range(first, last)])


def fresnel_tables(patch_width):
    freq = jnp.arange(patch_width, dtype=jnp.int32)
    signed = jnp.where(freq < patch_width // 2, freq, freq - patch_width).astype(jnp.float32)
    phases = math.pi * signed * signed / (4.0 * patch_width)
    product = freq[:, None] * freq[None, :] % patch_width
    angles = 2.0 * math.pi * product.astype(jnp.float32) / patch_width
    cos_table = jnp.cos(angles)
    sin_table = jnp.sin(angles)
    shifted_real = jnp.cos(angles - phases[None, :])
    shifted_imag = jnp.sin(angles - phases[None, :])
    highest = lax.Precision.HIGHEST
    prop_real = (
        jnp.dot(shifted_real, cos_table, precision=highest)
        + jnp.dot(shifted_imag, sin_table, precision=highest)
    ) / patch_width
    prop_imag = (
        jnp.dot(shifted_imag, cos_table, precision=highest)
        - jnp.dot(shifted_real, sin_table, precision=highest)
    ) / patch_width
    factor = 1.0 / math.sqrt(patch_width)
    far_real = cos_table * factor
    far_imag = -sin_table * factor
    return (prop_real, prop_imag, far_real, far_imag)


def left_product(mat_real, mat_imag, real_part, imag_part):
    width = mat_real.shape[0]
    stacked = jnp.concatenate(
        [
            jnp.concatenate([mat_real, -mat_imag], axis=1),
            jnp.concatenate([mat_imag, mat_real], axis=1),
        ],
        axis=0,
    )
    values = jnp.concatenate([real_part, imag_part], axis=-2)
    result = jnp.einsum("ab,...bc->...ac", stacked, values, precision=lax.Precision.HIGHEST)
    return (result[..., :width, :], result[..., width:, :])


def right_product(real_part, imag_part, mat_real, mat_imag):
    width = mat_real.shape[1]
    stacked = jnp.concatenate(
        [
            jnp.concatenate([mat_real, mat_imag], axis=1),
            jnp.concatenate([-mat_imag, mat_real], axis=1),
        ],
        axis=0,
    )
    values = jnp.concatenate([real_part, imag_part], axis=-1)
    result = jnp.einsum("...ab,bc->...ac", values, stacked, precision=lax.Precision.HIGHEST)
    return (result[..., :width], result[..., width:])


def apply_forward(mat_real, mat_imag, real_part, imag_part):
    left_real, left_imag = left_product(mat_real, mat_imag, real_part, imag_part)
    return right_product(left_real, left_imag, mat_real.T, mat_imag.T)


def apply_adjoint(mat_real, mat_imag, real_part, imag_part):
    left_real, left_imag = left_product(mat_real.T, -mat_imag.T, real_part, imag_part)
    return right_product(left_real, left_imag, mat_real, -mat_imag)


def complex_times(first_real, first_imag, second_real, second_imag):
    return (
        first_real * second_real - first_imag * second_imag,
        first_real * second_imag + first_imag * second_real,
    )


def conj_times(first_real, first_imag, second_real, second_imag):
    return (
        first_real * second_real + first_imag * second_imag,
        first_real * second_imag - first_imag * second_real,
    )


def on_device(transmission, illumination, measured, offsets, live_count):
    cut_index = lax.axis_index("cuts")
    cut_count = lax.axis_size("cuts")
    slot_count = measured.shape[0]
    patch_width = illumination.shape[-1]
    slice_depth = transmission.shape[1]
    tile_rows = transmission.shape[2]
    prop_real, prop_imag, far_real, far_imag = fresnel_tables(patch_width)
    border = shifted(transmission, "tile", -1)
    extended = jnp.concatenate([transmission, border], axis=2)
    anchor = jnp.zeros((), jnp.int32)

    def cut_patch(row_offset, col_offset):
        return lax.dynamic_slice(
            extended,
            (anchor, anchor, row_offset, col_offset),
            (2, slice_depth, patch_width, patch_width),
        )

    patches = jax.vmap(cut_patch)(offsets[:, 0], offsets[:, 1])
    used_slots = live_count[0]
    live_flags = (jnp.arange(slot_count, dtype=jnp.int32) < used_slots).astype(jnp.float32)
    group_count = slot_count // slot_count
    cut_first = cut_index == 0
    cut_last = cut_index == cut_count - 1

    def forward_section(section_step, loop_state):
        arrived, kept_waves, exit_grad = loop_state
        micro_batch = section_step - cut_index
        active = (
            (micro_batch >= 0)
            & (micro_batch < group_count)
            & (micro_batch * slot_count < used_slots)
        )
        first_slot = jnp.clip(micro_batch, 0, group_count - 1) * slot_count

        def forward_compute_section(unused):
            incoming = arrived.astype(jnp.float32)
            wave_real = jnp.where(cut_first, illumination[0], incoming[:, 0])
            wave_imag = jnp.where(cut_first, illumination[1], incoming[:, 1])
            saved_list = [jnp.stack([wave_real, wave_imag], axis=1)]
            chi_real, chi_imag = complex_times(
                wave_real, wave_imag, patches[:, 0, 0], patches[:, 1, 0]
            )
            wave_real, wave_imag = apply_forward(prop_real, prop_imag, chi_real, chi_imag)
            kept_new = lax.dynamic_update_slice_in_dim(
                kept_waves, jnp.stack(saved_list, axis=1), first_slot, 0
            )

            def far_side(unused_far):
                out_real, out_imag = apply_forward(far_real, far_imag, wave_real, wave_imag)
                weight = (out_real * out_real + out_imag * out_imag - measured) * live_flags[
                    :, None, None
                ]
                back_real, back_imag = apply_adjoint(
                    far_real, far_imag, weight * out_real, weight * out_imag
                )
                return jnp.stack([back_real, back_imag], axis=1)

            def skip_far(unused_far):
                return jnp.zeros((slot_count, 2, patch_width, patch_width), jnp.float32)

            grad_group = lax.cond(cut_last, far_side, skip_far, None)
            outgoing = jnp.stack([wave_real, wave_imag], axis=1).astype(jnp.bfloat16)
            return (outgoing, kept_new, grad_group)

        def forward_pass_through(unused):
            return (jnp.zeros_like(arrived), kept_waves, exit_grad)

        outgoing, kept_waves, exit_grad = lax.cond(
            active, forward_compute_section, forward_pass_through, None
        )
        arrived = passed_along(outgoing, "cuts", 1)
        return (arrived, kept_waves, exit_grad)

    start_state = (
        jnp.zeros((slot_count, 2, patch_width, patch_width), jnp.bfloat16),
        jnp.zeros((slot_count, slice_depth, 2, patch_width, patch_width), jnp.float32),
        jnp.zeros((slot_count, 2, patch_width, patch_width), jnp.float32),
    )
    unused_wave, kept_waves, exit_grad = lax.fori_loop(
        0, cut_count + group_count - 1, forward_section, start_state
    )

    def backward_section(section_step, loop_state):
        arrived, patch_grads = loop_state
        micro_batch = section_step - (cut_count - 1 - cut_index)
        active = (
            (micro_batch >= 0)
            & (micro_batch < group_count)
            & (micro_batch * slot_count < used_slots)
        )
        first_slot = jnp.clip(micro_batch, 0, group_count - 1) * slot_count

        def backward_compute_section(unused):
            grad_wave = jnp.where(cut_last, exit_grad, arrived.astype(jnp.float32))
            grad_real = grad_wave[:, 0]
            grad_imag = grad_wave[:, 1]
            pieces = [None] * slice_depth
            for layer_index in reversed(range(slice_depth)):
                chi_real, chi_imag = apply_adjoint(prop_real, prop_imag, grad_real, grad_imag)
                pieces[layer_index] = jnp.stack(
                    conj_times(
                        kept_waves[:, layer_index, 0],
                        kept_waves[:, layer_index, 1],
                        chi_real,
                        chi_imag,
                    ),
                    axis=1,
                )
                grad_real, grad_imag = conj_times(
                    patches[:, 0, layer_index], patches[:, 1, layer_index], chi_real, chi_imag
                )
            grads_new = lax.dynamic_update_slice_in_dim(
                patch_grads, jnp.stack(pieces, axis=2), first_slot, 0
            )
            outgoing = jnp.stack([grad_real, grad_imag], axis=1).astype(jnp.bfloat16)
            return (outgoing, grads_new)

        def backward_pass_through(unused):
            return (jnp.zeros_like(arrived), patch_grads)

        outgoing, patch_grads = lax.cond(
            active, backward_compute_section, backward_pass_through, None
        )
        arrived = passed_along(outgoing, "cuts", -1)
        return (arrived, patch_grads)

    back_state = (
        jnp.zeros((slot_count, 2, patch_width, patch_width), jnp.bfloat16),
        jnp.zeros_like(patches),
    )
    unused_grad, patch_grads = lax.fori_loop(
        0, cut_count + group_count - 1, backward_section, back_state
    )

    def add_patch(slot_index, total):
        corner = (anchor, anchor, offsets[slot_index, 0], offsets[slot_index, 1])
        current = lax.dynamic_slice(total, corner, (2, slice_depth, patch_width, patch_width))
        return lax.dynamic_update_slice(total, current + patch_grads[slot_index], corner)

    summed = lax.fori_loop(0, slot_count, add_patch, jnp.zeros_like(extended))
    spill = shifted(summed[:, :, tile_rows:, :].astype(jnp.bfloat16), "tile", 1).astype(jnp.float32)
    own_rows = summed[:, :, :tile_rows, :]
    return jnp.concatenate([own_rows + spill, own_rows[:, :, patch_width:, :]], axis=2)


def solution(mesh):
    placed = (P(None, "cuts", "tile", None), P(), P("tile", None, None), P("tile", None), P("tile"))
    return jax.shard_map(
        on_device,
        mesh=mesh,
        in_specs=placed,
        out_specs=P(None, "cuts", "tile", None),
        check_vma=False,
    )
```

profile of v0, /device:TPU:1, one launch (start us, length us, event | category | flops | bytes accessed | tf_op | source)
XLA Modules:
  0.0 120.5 jit_solution(6771761750297009781)
XLA Ops:
  0.0 11.0 %collective-permute-start.2 = (f32[2,1,256,512]{3,2,1,0:T(8,128)}, f32[2,1,256,512]{3,2,1,0:T(8,128)S(1)}, u32[]{:S(2)}, u32[]{:S(2)}) collective-permute-start(f32[2,1,256,512]{3,2,1,0:T(8,128)} %param.15), channel_id=1, source_target_pairs={{0,127},{1,0},{2,1},{3,2},{4,3},{5,4},{6,5},{7,6},{8,7},{9,8},{10,... | collective-permute-start | bytes 3145736 | tf_op jit(solution)/shard_map/ppermute | solution.py:12
  11.0 1.3 %fusion.130 = (s32[1,1]{1,0:T(1,128)}, s32[1,1]{1,0:T(1,128)}) fusion(s32[1,2]{1,0:T(1,128)} %param.18), kind=kLoop, calls=%fused_computation.184 | loop fusion | bytes 16 | tf_op jit(solution)/shard_map/slice | solution.py:117
  20.7 2.2 %fusion.90 = f32[256,256]{1,0:T(8,128)S(1)} fusion(f32[256]{0:T(256)S(1)} %fusion.105), kind=kOutput, calls=%fused_computation.152 | convolution fusion | flops 203227136 | bytes 263168 | tf_op jit(solution)/shard_map/dot_general | solution.py:33
  22.9 2.2 %fusion.89 = f32[256,256]{1,0:T(8,128)S(1)} fusion(f32[256]{0:T(256)S(1)} %fusion.105), kind=kOutput, calls=%fused_computation.151 | convolution fusion | flops 203227136 | bytes 263168 | tf_op jit(solution)/shard_map/dot_general | solution.py:37
  25.1 2.9 %fusion.79 = f32[256,256]{1,0:T(8,128)} fusion(f32[256,256]{1,0:T(8,128)S(1)} %fusion.90, f32[256]{0:T(256)S(1)} %fusion.105), kind=kOutput, calls=%fused_computation.133 | convolution fusion | flops 203358208 | bytes 525312 | tf_op jit(solution)/shard_map/dot_general | solution.py:34
  28.0 2.2 %fusion.80 = f32[256,256]{1,0:T(8,128)S(1)} fusion(f32[256,256]{1,0:T(8,128)S(1)} %fusion.89, f32[256]{0:T(256)S(1)} %fusion.105), kind=kOutput, calls=%fused_computation.135 | convolution fusion | flops 203358208 | bytes 525312 | tf_op jit(solution)/shard_map/dot_general | solution.py:38
  30.2 3.0 %collective-permute-done.2 = f32[2,1,256,512]{3,2,1,0:T(8,128)S(1)} collective-permute-done((f32[2,1,256,512]{3,2,1,0:T(8,128)}, f32[2,1,256,512]{3,2,1,0:T(8,128)S(1)}, u32[]{:S(2)}, u32[]{:S(2)}) %collective-permute-start.2) | collective-permute-done | bytes 1048608 | tf_op jit(solution)/shard_map/ppermute | solution.py:12
  34.5 35.2 %while.46 = (s32[]{:T(128)}, bf16[1,2,256,256]{3,2,1,0:T(8,128)(2,1)S(1)}, f32[1,1,2,256,256]{4,3,2,1,0:T(8,128)S(1)}, f32[1,2,256,256]{3,2,1,0:T(8,128)}, s32[]...) while((s32[]{:T(128)}, ...), condition=%wide.region_5.6_spmd.clone.clone, body=%wide.region_0.5_spmd.clone.clone.sunk | while | flops 4840226816 | bytes 30933484 | solution.py:178
  35.5 1.3 %collective-permute-start.1 = (bf16[1,2,256,256]{3,2,1,0:T(8,128)(2,1)S(1)}, bf16[1,2,256,256]{3,2,1,0:T(8,128)(2,1)S(1)}, u32[]{:S(2)}, u32[]{:S(2)}) collective-permute-start(bf16[1,2,256,256]{3,2,1,0:T(8,128)(2,1)S(1)} %get-tuple-element.1063), channel_id=1, source_target_pairs={{0,128},{1,129},{2,130},{3,131},{4,132},{5,133},{6,134},{7,135},{8... | collective-permute-start | bytes 786440 | tf_op jit(solution)/shard_map/while/body/eval_jaxpr/ppermute | solution.py:18
  36.8 12.4 %collective-permute-done.1 = bf16[1,2,256,256]{3,2,1,0:T(8,128)(2,1)S(1)} collective-permute-done((bf16[1,2,256,256]{3,2,1,0:T(8,128)(2,1)S(1)}, bf16[1,2,256,256]{3,2,1,0:T(8,128)(2,1)S(1)}, u32[]{:S(2)}, u32[]{:S(2)}) %collective-permute-start.1) | collective-permute-done | bytes 262176 | tf_op jit(solution)/shard_map/while/body/eval_jaxpr/ppermute | solution.py:18
  50.1 16.1 %conditional.9 = (bf16[1,2,256,256]{3,2,1,0:T(8,128)(2,1)S(1)}, f32[1,1,2,256,256]{4,3,2,1,0:T(8,128)S(1)}, f32[1,2,256,256]{3,2,1,0:T(8,128)}) conditional(s32[]{:T(128)} %convert_element_type.149, (f32[1,1,2,256,256]{4,3,2,1,0:T(8,128)S(1)}, f32[1,2,256,256]{3,2,1,0:T(8,128)}) %tuple.135, (pred[]{:T(512)}, f32[2,256,256]{2,1,0:T(8,128)}, ...), branch_computations={%region_1.1_spmd, %region_2.4_spmd.clone} | conditional | flops 4839309312 | bytes 29360250 | solution.py:167
  50.2 1.1 fusion.69
  51.4 2.9 %convolution_bitcast_fusion.7 = f32[1,512,256]{1,2,0:T(8,128)S(1)} fusion(f32[256,256]{1,0:T(8,128)} %get-tuple-element.801, f32[256,256]{1,0:T(8,128)S(1)} %get-tuple-element.802, f32[256,256]{1,0:T(8,128)S(1)} %neg.41, f32[1,256,256]{2,1,0:T(8,128)S(1)} %fusion.70, f32[1,256,256]{2,1,0:T(8,128)S(1)} %get-tuple-element.873), kind=kOutput, calls=%fused_computation.80 | convolution fusion | flops 806223872 | bytes 1835008 | tf_op jit(solution)/shard_map/while/body/eval_jaxpr/cond/branch_1_fun/ab,...bc->...ac/dot_general | solution.py:56
  54.4 2.9 %convolution_bitcast_fusion.6 = f32[1,256,512]{2,1,0:T(8,128)S(1)} fusion(f32[256,256]{0,1:T(8,128)} %bitcast.69, f32[256,256]{0,1:T(8,128)S(1)} %bitcast_negate_fusion.2, f32[256,256]{0,1:T(8,128)S(1)} %bitcast.177, f32[1,256,256]{1,2,0:T(8,128)S(1)} %get-tuple-element.899, f32[1,256,256]{1,2,0:T(8,128)S(1)} %get-tuple-element.898), kind=kOutput, calls=%fused_computation.79 | convolution fusion | flops 806223872 | bytes 1835008 | tf_op jit(solution)/shard_map/while/body/eval_jaxpr/cond/branch_1_fun/...ab,bc->...ac/dot_general | solution.py:70
  57.3 1.7 %fusion.68 = (f32[256,256]{1,0:T(8,128)S(1)}, f32[256,256]{1,0:T(8,128)S(1)}) fusion(f32[256,256]{1,0:T(8,128)S(1)} %get-tuple-element.807, f32[256,256]{1,0:T(8,128)S(1)} %get-tuple-element.808, f32[256,256]{1,0:T(8,128)S(1)} %get-tuple-element.807, f32[256,256]{1,0:T(8,128)S(1)} %get-tuple-element.808), kind=kLoop, calls=%fused_computation.108 | loop fusion | flops 196608 | bytes 1572864 | tf_op jit(solution)/shard_map/mul | solution.py:42
  59.1 7.0 %conditional.5 = (f32[1,2,256,256]{3,2,1,0:T(8,128)}) conditional(s32[]{:T(128)} %convert_element_type.112, () %tuple.94, (f32[1,256,256]{2,1,0:T(8,128)S(1)}, f32[1,256,256]{2,1,0:T(8,128)S(1)}, f32[256,256]{1,0:T(8,128)S(1)}, f32[256,256]{1,0:T(8,128)S(1)}, f32[256,256]{1,0:T(8,128)S(1)}, /*index=5*/f32[256,256]{1,0:T(8,128)S(1)}, ...), branch_computations={%region_3.2_spmd, %region_4.3_spmd} | conditional | flops 3225616384 | bytes 14417932 | solution.py:160
  59.1 1.9 %convolution_bitcast_fusion.3 = f32[1,512,256]{1,2,0:T(8,128)S(1)} fusion(f32[256,256]{1,0:T(8,128)S(1)} %get-tuple-element.631, f32[256,256]{1,0:T(8,128)S(1)} %get-tuple-element.632, f32[256,256]{1,0:T(8,128)S(1)} %neg.26, f32[256,256]{1,0:T(8,128)S(1)} %get-tuple-element.631, f32[1,256,256]{2,1,0:T(8,128)S(1)} %get-tuple-element.626, ...), kind=kOutput, calls=%fused_computation.5 | convolution fusion | flops 806223872 | bytes 2097152 | tf_op jit(solution)/shard_map/while/body/eval_jaxpr/cond/branch_1_fun/cond/branch_1_fun/ab,...bc->...ac/dot_general | solution.py:56
  61.1 1.9 %convolution_bitcast_fusion.2 = f32[1,256,512]{2,1,0:T(8,128)S(1)} fusion(f32[256,256]{0,1:T(8,128)S(1)} %bitcast.183, f32[256,256]{0,1:T(8,128)S(1)} %bitcast_negate_fusion, f32[256,256]{0,1:T(8,128)S(1)} %bitcast.181, f32[1,256,256]{1,2,0:T(8,128)S(1)} %get-tuple-element.883, f32[1,256,256]{1,2,0:T(8,128)S(1)} %get-tuple-element.882), kind=kOutput, calls=%fused_computation.4 | convolution fusion | flops 806223872 | bytes 1835008 | tf_op jit(solution)/shard_map/while/body/eval_jaxpr/cond/branch_1_fun/cond/branch_1_fun/...ab,bc->...ac/dot_general | solution.py:70
  66.2 1.3 %collective-permute-start.1 = (bf16[1,2,256,256]{3,2,1,0:T(8,128)(2,1)S(1)}, bf16[1,2,256,256]{3,2,1,0:T(8,128)(2,1)S(1)}, u32[]{:S(2)}, u32[]{:S(2)}) collective-permute-start(bf16[1,2,256,256]{3,2,1,0:T(8,128)(2,1)S(1)} %get-tuple-element.1063), channel_id=1, source_target_pairs={{0,128},{1,129},{2,130},{3,131},{4,132},{5,133},{6,134},{7,135},{8... | collective-permute-start | bytes 786440 | tf_op jit(solution)/shard_map/while/body/eval_jaxpr/ppermute | solution.py:18
  67.5 2.1 %collective-permute-done.1 = bf16[1,2,256,256]{3,2,1,0:T(8,128)(2,1)S(1)} collective-permute-done((bf16[1,2,256,256]{3,2,1,0:T(8,128)(2,1)S(1)}, bf16[1,2,256,256]{3,2,1,0:T(8,128)(2,1)S(1)}, u32[]{:S(2)}, u32[]{:S(2)}) %collective-permute-start.1) | collective-permute-done | bytes 262176 | tf_op jit(solution)/shard_map/while/body/eval_jaxpr/ppermute | solution.py:18
  69.7 17.8 %while.45 = (s32[]{:T(128)}, bf16[1,2,256,256]{3,2,1,0:T(8,128)(2,1)S(1)}, f32[1,2,1,256,256]{4,3,1,2,0:T(8,128)S(1)}, s32[]{:T(128)}, s32[]{:T(128)}, /*index=5...) while((s32[]{:T(128)}, ...), condition=%wide.region_9.10_spmd, body=%wide.region_6.9_spmd.sunk | while | flops 1614020608 | bytes 13107488 | solution.py:230
  70.6 5.7 %conditional.8 = (bf16[1,2,256,256]{3,2,1,0:T(8,128)(2,1)S(1)}, f32[1,2,1,256,256]{4,3,1,2,0:T(8,128)S(1)}) conditional(s32[]{:T(128)} %convert_element_type.147, f32[1,2,1,256,256]{4,3,1,2,0:T(8,128)S(1)} %get-tuple-element.1142, (f32[1,2,1,256,256]{4,3,2,1,0:T(8,128)S(1)}, pred[]{:T(512)}, bf16[1,2,256,256]{3,2,1,0:T(8,128)(2,1)S(1)}, ...), branch_computations={%region_7.7_spmd, %region_8.8_spmd} | conditional | flops 1614020608 | bytes 12058641 | solution.py:220
  70.7 1.1 convert_select_fusion
  71.8 2.1 %convolution_bitcast_fusion.5 = f32[1,512,256]{1,2,0:T(8,128)S(1)} fusion(f32[256,256]{0,1:T(8,128)} %bitcast.38, f32[256,256]{0,1:T(8,128)S(1)} %bitcast_negate_fusion.1, f32[256,256]{0,1:T(8,128)S(1)} %bitcast.178, f32[1,256,256]{2,1,0:T(8,128)S(1)} %get-tuple-element.893, f32[1,256,256]{2,1,0:T(8,128)S(1)} %get-tuple-element.892), kind=kOutput, calls=%fused_computation.32 | convolution fusion | flops 806223872 | bytes 1835008 | tf_op jit(solution)/shard_map/while/body/eval_jaxpr/cond/branch_1_fun/ab,...bc->...ac/dot_general | solution.py:56
  74.0 2.1 %convolution_bitcast_fusion.4 = f32[1,256,512]{2,1,0:T(8,128)S(1)} fusion(f32[256,256]{1,0:T(8,128)} %get-tuple-element.678, f32[256,256]{1,0:T(8,128)S(1)} %get-tuple-element.679, f32[256,256]{1,0:T(8,128)S(1)} %neg.31, f32[1,256,256]{1,2,0:T(8,128)S(1)} %get-tuple-element.891, f32[1,256,256]{1,2,0:T(8,128)S(1)} %get-tuple-element.890), kind=kOutput, calls=%fused_computation.31 | convolution fusion | flops 806223872 | bytes 1835008 | tf_op jit(solution)/shard_map/while/body/eval_jaxpr/cond/branch_1_fun/...ab,bc->...ac/dot_general | solution.py:70
  76.3 1.3 %collective-permute-start = (bf16[1,2,256,256]{3,2,1,0:T(8,128)(2,1)S(1)}, bf16[1,2,256,256]{3,2,1,0:T(8,128)(2,1)S(1)}, u32[]{:S(2)}, u32[]{:S(2)}) collective-permute-start(bf16[1,2,256,256]{3,2,1,0:T(8,128)(2,1)S(1)} %get-tuple-element.1047), channel_id=1, source_target_pairs={{128,0},{129,1},{130,2},{131,3},{132,4},{133,5},{134,6},{135,7},{1... | collective-permute-start | bytes 786440 | tf_op jit(solution)/shard_map/while/body/eval_jaxpr/ppermute | solution.py:18
  77.6 1.1 collective-permute-done
  79.4 6.9 %collective-permute-start = (bf16[1,2,256,256]{3,2,1,0:T(8,128)(2,1)S(1)}, bf16[1,2,256,256]{3,2,1,0:T(8,128)(2,1)S(1)}, u32[]{:S(2)}, u32[]{:S(2)}) collective-permute-start(bf16[1,2,256,256]{3,2,1,0:T(8,128)(2,1)S(1)} %get-tuple-element.1047), channel_id=1, source_target_pairs={{128,0},{129,1},{130,2},{131,3},{132,4},{133,5},{134,6},{135,7},{1... | collective-permute-start | bytes 786440 | tf_op jit(solution)/shard_map/while/body/eval_jaxpr/ppermute | solution.py:18
  86.3 1.1 collective-permute-done
  89.3 10.0 %dynamic_update_slice.6 = f32[2,1,512,512]{3,2,1,0:T(8,128)S(1)} dynamic-update-slice(f32[2,1,512,512]{3,2,1,0:T(8,128)S(1)} %broadcast_in_dim.23, f32[2,1,256,256]{3,2,1,0:T(8,128)S(1)} %bitcast.185, s32[]{:T(128)} %constant.97.clone.1, s32[]{:T(128)} %constant.97.clone.1, s32[]{:T(128)S(6)} %select_n.98, s32[]{:T(128)S(6)} %select_n.99) | dynamic-update-slice | bytes 1048580 | tf_op jit(solution)/shard_map/while/body/eval_jaxpr/dynamic_update_slice | solution.py:237
  99.5 19.8 %collective-permute-done.3 = bf16[2,1,256,512]{3,2,1,0:T(8,128)(2,1)S(1)} collective-permute-done((bf16[2,1,256,512]{3,2,1,0:T(8,128)(2,1)S(1)}, bf16[2,1,256,512]{3,2,1,0:T(8,128)(2,1)S(1)}, u32[]{:S(2)}, u32[]{:S(2)}) %collective-permute-start.3) | collective-permute-done | bytes 524320 | tf_op jit(solution)/shard_map/ppermute | solution.py:12
  119.3 1.1 slice_add_fusion
  (51 shorter events, 7.5 us)
Async XLA Ops:
  0.0 33.2 %collective-permute-start.2 = (f32[2,1,256,512]{3,2,1,0:T(8,128)}, f32[2,1,256,512]{3,2,1,0:T(8,128)S(1)}, u32[]{:S(2)}, u32[]{:S(2)}) collective-permute-start(f32[2,1,256,512]{3,2,1,0:T(8,128)} %param.15), channel_id=1, source_target_pairs={{0,127},{1,0},{2,1},{3,2},{4,3},{5,4},{6,5},{7,6},{8,7},{9,8},{10,... | collective-permute-start | bytes 3145736 | tf_op jit(solution)/shard_map/ppermute | solution.py:12
  25.1 8.1 %copy-start.3 = (f32[2,1,256,512]{3,2,1,0:T(8,128)S(1)}, f32[2,1,256,512]{3,2,1,0:T(8,128)}, u32[]{:S(2)}) copy-start(f32[2,1,256,512]{3,2,1,0:T(8,128)} %param.15) | copy-start | bytes 3145732
  30.2 4.2 %copy-start = (f32[1,256,256]{2,1,0:T(8,128)S(1)}, f32[1,256,256]{2,1,0:T(8,128)}, u32[]{:S(2)}) copy-start(f32[1,256,256]{2,1,0:T(8,128)} %param.17) | copy-start | bytes 786436
  35.5 13.7 %collective-permute-start.1 = (bf16[1,2,256,256]{3,2,1,0:T(8,128)(2,1)S(1)}, bf16[1,2,256,256]{3,2,1,0:T(8,128)(2,1)S(1)}, u32[]{:S(2)}, u32[]{:S(2)}) collective-permute-start(bf16[1,2,256,256]{3,2,1,0:T(8,128)(2,1)S(1)} %get-tuple-element.1063), channel_id=1, source_target_pairs={{0,128},{1,129},{2,130},{3,131},{4,132},{5,133},{6,134},{7,135},{8... | collective-permute-start | bytes 786440 | tf_op jit(solution)/shard_map/while/body/eval_jaxpr/ppermute | solution.py:18
  66.2 3.4 %collective-permute-start.1 = (bf16[1,2,256,256]{3,2,1,0:T(8,128)(2,1)S(1)}, bf16[1,2,256,256]{3,2,1,0:T(8,128)(2,1)S(1)}, u32[]{:S(2)}, u32[]{:S(2)}) collective-permute-start(bf16[1,2,256,256]{3,2,1,0:T(8,128)(2,1)S(1)} %get-tuple-element.1063), channel_id=1, source_target_pairs={{0,128},{1,129},{2,130},{3,131},{4,132},{5,133},{6,134},{7,135},{8... | collective-permute-start | bytes 786440 | tf_op jit(solution)/shard_map/while/body/eval_jaxpr/ppermute | solution.py:18
  76.3 2.4 %collective-permute-start = (bf16[1,2,256,256]{3,2,1,0:T(8,128)(2,1)S(1)}, bf16[1,2,256,256]{3,2,1,0:T(8,128)(2,1)S(1)}, u32[]{:S(2)}, u32[]{:S(2)}) collective-permute-start(bf16[1,2,256,256]{3,2,1,0:T(8,128)(2,1)S(1)} %get-tuple-element.1047), channel_id=1, source_target_pairs={{128,0},{129,1},{130,2},{131,3},{132,4},{133,5},{134,6},{135,7},{1... | collective-permute-start | bytes 786440 | tf_op jit(solution)/shard_map/while/body/eval_jaxpr/ppermute | solution.py:18
  79.4 8.0 %collective-permute-start = (bf16[1,2,256,256]{3,2,1,0:T(8,128)(2,1)S(1)}, bf16[1,2,256,256]{3,2,1,0:T(8,128)(2,1)S(1)}, u32[]{:S(2)}, u32[]{:S(2)}) collective-permute-start(bf16[1,2,256,256]{3,2,1,0:T(8,128)(2,1)S(1)} %get-tuple-element.1047), channel_id=1, source_target_pairs={{128,0},{129,1},{130,2},{131,3},{132,4},{133,5},{134,6},{135,7},{1... | collective-permute-start | bytes 786440 | tf_op jit(solution)/shard_map/while/body/eval_jaxpr/ppermute | solution.py:18
  87.5 0.8 copy-start.1
  88.3 1.0 copy-start.2
  99.4 19.9 %collective-permute-start.3 = (bf16[2,1,256,512]{3,2,1,0:T(8,128)(2,1)S(1)}, bf16[2,1,256,512]{3,2,1,0:T(8,128)(2,1)S(1)}, u32[]{:S(2)}, u32[]{:S(2)}) collective-permute-start(bf16[2,1,256,512]{3,2,1,0:T(8,128)(2,1)S(1)} %slice.232), channel_id=1, source_target_pairs={{0,1},{1,2},{2,3},{3,4},{4,5},{5,6},{6,7},{7,8},{8,9},{9,10},{10,1... | collective-permute-start | bytes 1572872 | tf_op jit(solution)/shard_map/ppermute | solution.py:12
where the time goes:
time: 119 us; the launch traced here: 120 us
  waiting for transfers between devices  39.6 us (33%)
  matrix products  25.3 us (21%)
  starting transfers between devices  21.9 us (18%)
  local copies, waits for them, and re-layouts  14.5 us (12%)
  between operations  8.45 us (7%)
  other arithmetic  7.14 us (6%)
  loops' own time  3.53 us (3%)
    ppermute x2, waiting for transfers between devices, shifted(): return lax.ppermute(value, axis, pairs)  22.8 us
    ppermute x4, waiting for transfers between devices, passed_along(): lax.ppermute(value, axis, [(source, source + steps) for source in range(f...  16.8 us
    ppermute x2, starting transfers between devices, shifted(): return lax.ppermute(value, axis, pairs)  11.1 us
    ppermute x4, starting transfers between devices, passed_along(): lax.ppermute(value, axis, [(source, source + steps) for source in range(f...  10.8 us
    dynamic_update_slice x1, local copies, waits for them, and re-layouts, add_patch(): lax.dynamic_update_slice(total, current + patch_grads[slot_index], corner)  10 us
    dot_general x4, matrix products, left_product(): jnp.einsum('ab,...bc->...ac', stacked, values, precision=lax.Precision.HI...  7.91 us
    dot_general x4, matrix products, right_product(): jnp.einsum('...ab,bc->...ac', values, stacked, precision=lax.Precision.HI...  7.91 us
    dot_general x1, matrix products, fresnel_tables(): jnp.dot(shifted_imag, sin_table, precision=highest)  2.9 us
  transfers between devices with their start and end apart: 6, of which 6 were waited for; matrix products, arithmetic and copies ran while one was open for 9% of the time, Pallas kernels for 0%

commit v1 on v0

v1 whole, which is shorter than its diff:
```python
import functools
import math

import jax
import jax.numpy as jnp
import numpy as np
from jax import lax
from jax.experimental import pallas as pl
from jax.experimental.pallas import tpu as pltpu
from jax.sharding import PartitionSpec as P

W = 256
HEAD = 16
TOP = 32000.0
MEASURED_STEP = 5.0 / TOP
VMEM = pl.BlockSpec(memory_space=pltpu.VMEM)
SMEM = pl.BlockSpec(memory_space=pltpu.SMEM)


def split_table(matrix):
    parts = []
    for factor in (matrix.real, matrix.imag - matrix.real, matrix.real + matrix.imag):
        factor = np.asarray(factor, np.float32)
        high = factor.astype(jnp.bfloat16)
        low = (factor - high.astype(np.float32)).astype(jnp.bfloat16)
        parts += [high, low]
    return np.stack(parts)


@functools.lru_cache(None)
def tables():
    freq = np.arange(W)
    signed = np.where(freq < W // 2, freq, freq - W).astype(np.float64)
    phase = np.pi * signed * signed / (4 * W)
    basis = np.exp(2j * np.pi * ((freq[:, None] * freq[None, :]) % W) / W)
    prop = (basis * np.exp(-1j * phase)[None, :]) @ np.conj(basis).T / W
    far = np.conj(basis) / math.sqrt(W)
    return split_table(prop), split_table(far)


def halves(value):
    high = value.astype(jnp.bfloat16)
    low = (value - high.astype(jnp.float32)).astype(jnp.bfloat16)
    return high, low


def dot(first, second):
    return jnp.dot(first, second, preferred_element_type=jnp.float32)


def right(value, table, which):
    high, low = halves(value)
    big, small = table[2 * which], table[2 * which + 1]
    return dot(high, big) + dot(low, big) + dot(high, small)


def left(value, table, which):
    high, low = halves(value)
    big, small = table[2 * which], table[2 * which + 1]
    return dot(big, high) + dot(big, low) + dot(small, high)


def product(times, real, imag, table, conj):
    both = times(real + imag, table, 0)
    if conj:
        return both + times(imag, table, 1), both - times(real, table, 2)
    return both - times(imag, table, 2), both + times(real, table, 1)


def transform(real, imag, table, conj):
    real, imag = product(right, real, imag, table, conj)
    return product(left, real, imag, table, conj)


def iota(dim):
    return lax.broadcasted_iota(jnp.int32, (W, W), dim)


def windowed(full, part, col):
    return jnp.where(iota(1) >= col, full[part, :, :W], full[part, :, W:])


def encode_kernel(offsets, own, measured, coded, coded_measured):
    col = offsets[0, 1]
    real = windowed(own.at[:, 0], 0, col)
    imag = windowed(own.at[:, 0], 1, col)
    peak = jnp.max(jnp.maximum(jnp.abs(real), jnp.abs(imag)), axis=0, keepdims=True)
    peak = jnp.max(peak, axis=1, keepdims=True)
    peak = jnp.broadcast_to(jnp.maximum(peak, 1e-30), (1, W))
    power = jnp.ceil(jnp.log(peak) * (1.0 / math.log(2.0)))
    gain = jnp.exp2(-power) * TOP
    coded[0, :W, :] = jnp.round(real * gain).astype(jnp.int32).astype(jnp.int16)
    coded[1, :W, :] = jnp.round(imag * gain).astype(jnp.int32).astype(jnp.int16)
    head = jnp.broadcast_to(power.astype(jnp.int32), (HEAD, W)).astype(jnp.int16)
    coded[0, W:, :] = head
    coded[1, W:, :] = head
    scaled = jnp.round(measured[0] * (1.0 / MEASURED_STEP))
    coded_measured[...] = scaled.astype(jnp.int32).astype(jnp.int16)


def decoded(coded, part):
    power = coded[0, W : W + HEAD, :].astype(jnp.int32).astype(jnp.float32)[0:1]
    step = jnp.exp2(power) * (1.0 / TOP)
    return coded[part, :W, :].astype(jnp.int32).astype(jnp.float32) * step


def patch_of(coded, own, row, col, part):
    return jnp.where(iota(0) >= row, decoded(coded, part), windowed(own, part, col))


def roll_kernel(offsets, illumination, rolled):
    row = lax.rem(offsets[0, 0], W)
    col = lax.rem(offsets[0, 1], W)
    for part in range(2):
        rolled[part] = pltpu.roll(pltpu.roll(illumination[part], row, 0), col, 1)


def first_kernel(offsets, coded, own, rolled, prop, psi):
    row, col = offsets[0, 0], offsets[0, 1]
    patch_real = patch_of(coded, own.at[:, 0], row, col, 0)
    patch_imag = patch_of(coded, own.at[:, 0], row, col, 1)
    wave_real, wave_imag = rolled[0], rolled[1]
    chi_real = wave_real * patch_real - wave_imag * patch_imag
    chi_imag = wave_real * patch_imag + wave_imag * patch_real
    out_real, out_imag = transform(chi_real, chi_imag, prop, False)
    psi[0] = out_real.astype(jnp.bfloat16)
    psi[1] = out_imag.astype(jnp.bfloat16)


def second_kernel(offsets, coded, other, psi, far, patch, field):
    row, col = offsets[0, 0], offsets[0, 1]
    patch_real = patch_of(coded, other, row, col, 0)
    patch_imag = patch_of(coded, other, row, col, 1)
    patch[0] = patch_real
    patch[1] = patch_imag
    wave_real, wave_imag = psi[0].astype(jnp.float32), psi[1].astype(jnp.float32)
    chi_real = wave_real * patch_real - wave_imag * patch_imag
    chi_imag = wave_real * patch_imag + wave_imag * patch_real
    out_real, out_imag = transform(chi_real, chi_imag, far, False)
    field[0] = out_real
    field[1] = out_imag


def third_kernel(live, coded_measured, field, psi, patch, far, grad, wave_grad):
    flag = (live[0] > 0).astype(jnp.float32)
    target = coded_measured[...].astype(jnp.int32).astype(jnp.float32) * MEASURED_STEP
    real, imag = field[0], field[1]
    weight = (real * real + imag * imag - target) * flag
    real, imag = transform(weight * real, weight * imag, far, True)
    wave_real, wave_imag = psi[0].astype(jnp.float32), psi[1].astype(jnp.float32)
    grad[0] = (wave_real * real + wave_imag * imag).astype(jnp.bfloat16)
    grad[1] = (wave_real * imag - wave_imag * real).astype(jnp.bfloat16)
    patch_real, patch_imag = patch[0], patch[1]
    wave_grad[0] = (patch_real * real + patch_imag * imag).astype(jnp.bfloat16)
    wave_grad[1] = (patch_real * imag - patch_imag * real).astype(jnp.bfloat16)


def fourth_kernel(wave_grad, rolled, prop, grad):
    real, imag = transform(wave_grad[0].astype(jnp.float32), wave_grad[1].astype(jnp.float32), prop, True)
    wave_real, wave_imag = rolled[0], rolled[1]
    grad[0] = (wave_real * real + wave_imag * imag).astype(jnp.bfloat16)
    grad[1] = (wave_real * imag - wave_imag * real).astype(jnp.bfloat16)


def place_kernel(offsets, before, core, own_first, own_second, spill_first, spill_second, out):
    row, col = offsets[0, 0], offsets[0, 1]
    row_before, col_before = before[0, 0], before[0, 1]

    def place(own, spill):
        for part in range(2):
            mine = jnp.where(iota(0) >= row, own[part].astype(jnp.float32), 0.0)
            theirs = jnp.where(iota(0) < row_before, spill[part].astype(jnp.float32), 0.0)
            out[part, 0, :, :W] = jnp.where(iota(1) >= col, mine, 0.0) + jnp.where(iota(1) >= col_before, theirs, 0.0)
            out[part, 0, :, W:] = jnp.where(iota(1) < col, mine, 0.0) + jnp.where(iota(1) < col_before, theirs, 0.0)

    @pl.when(core[0] == 0)
    def _():
        place(own_first, spill_first)

    @pl.when(core[0] != 0)
    def _():
        place(own_second, spill_second)


def call(kernel, outs, specs, name, mib=16):
    return pl.pallas_call(
        kernel,
        out_shape=outs,
        in_specs=specs,
        out_specs=jax.tree.map(lambda _: VMEM, outs),
        name=name,
        compiler_params=pltpu.CompilerParams(vmem_limit_bytes=mib << 20),
    )


def shaped(shape, dtype):
    return jax.ShapeDtypeStruct(shape, dtype)


def on_device(transmission, illumination, measured, offsets, live_count):
    prop, far = (jnp.asarray(t) for t in tables())
    count = lax.axis_size("tile")
    core = lax.axis_index("cuts").astype(jnp.int32)[None]
    axes = ("cuts", "tile")

    def hop(value, source, target, steps):
        pairs = [(source * count + k, target * count + (k + steps) % count) for k in range(count)]
        return lax.ppermute(value, axes, pairs)

    def both(value, steps):
        return lax.ppermute(value, "tile", [(k, (k + steps) % count) for k in range(count)])

    before = both(offsets, 1)
    live = both(live_count, 1)
    coded, coded_measured = call(
        encode_kernel,
        (shaped((2, W + HEAD, W), jnp.int16), shaped((W, W), jnp.int16)),
        [SMEM, VMEM, VMEM],
        "encode",
    )(offsets, transmission, measured)
    first_coded = hop(coded, 0, 0, 1)
    other = hop(transmission[:, 0], 1, 0, 0)
    second_coded = hop(coded, 1, 0, 1)
    target = hop(coded_measured, 1, 0, 1)
    rolled = call(roll_kernel, shaped((2, W, W), jnp.float32), [SMEM, VMEM], "roll")(before, illumination)
    psi = call(
        first_kernel, shaped((2, W, W), jnp.bfloat16), [SMEM, VMEM, VMEM, VMEM, VMEM], "first"
    )(before, first_coded, transmission, rolled, prop)
    patch, field = call(
        second_kernel,
        (shaped((2, W, W), jnp.float32), shaped((2, W, W), jnp.float32)),
        [SMEM, VMEM, VMEM, VMEM, VMEM],
        "second",
    )(before, second_coded, other, psi, far)
    grad_second, wave_grad = call(
        third_kernel,
        (shaped((2, W, W), jnp.bfloat16), shaped((2, W, W), jnp.bfloat16)),
        [SMEM, VMEM, VMEM, VMEM, VMEM, VMEM],
        "third",
    )(live, target, field, psi, patch, far)
    own_second = hop(grad_second, 0, 1, -1)
    spill_second = hop(grad_second, 0, 1, 0)
    grad_first = call(fourth_kernel, shaped((2, W, W), jnp.bfloat16), [VMEM, VMEM, VMEM], "fourth")(
        wave_grad, rolled, prop
    )
    own_first = hop(grad_first, 0, 0, -1)
    return call(
        place_kernel,
        shaped(transmission.shape, jnp.float32),
        [SMEM, SMEM, SMEM, VMEM, VMEM, VMEM, VMEM],
        "place",
    )(offsets, before, core, own_first, own_second, grad_first, spill_second)


def solution(mesh):
    placed = (P(None, "cuts", "tile", None), P(), P("tile", None, None), P("tile", None), P("tile"))
    return jax.shard_map(
        on_device,
        mesh=mesh,
        in_specs=placed,
        out_specs=P(None, "cuts", "tile", None),
        check_vma=False,
    )
```

time: 119 us -> 50.2 us (0.42); the launches traced: 120 us -> 49.8 us
  matrix products: 25.3 us -> 0 us
  waiting for transfers between devices: 39.6 us -> 21.4 us
  local copies, waits for them, and re-layouts: 14.5 us -> 3.23 us
  Pallas kernels: 0 us -> 10 us
  between operations: 8.45 us -> 0.2 us
  other arithmetic: 7.14 us -> 0 us
  starting transfers between devices: 21.9 us -> 15 us
  loops' own time: 3.53 us -> 0 us
    dot_general x12 -> x0, matrix products: 25.3 us -> none  [the longest x4 7.91 us: left_product(): jnp.einsum('ab,...bc->...ac', stacked, values, precision=lax.Precision.HI...]
    ppermute x6 -> x9, waiting for transfers between devices: 39.6 us -> 21.4 us  [the longest x2 14.8 us: both(): lax.ppermute(value, 'tile', [(k, (k + steps) % count) for k in range(coun...]
    pallas_call x0 -> x7, Pallas kernels: none -> 10 us  [the longest x1 1.99 us: on_device(): call(third_kernel, (shaped((2, W, W), jnp.bfloat16), shaped((2, W, W), jn...]
    dynamic_update_slice x1 -> x0, local copies, waits for them, and re-layouts: 10 us -> none  [add_patch(): lax.dynamic_update_slice(total, current + patch_grads[slot_index], corner)]
    ppermute x6 -> x9, starting transfers between devices: 21.9 us -> 15 us  [the longest x7 14 us: hop(): return lax.ppermute(value, axes, pairs)]
    another operation x7 -> x0, loops' own time: 3.53 us -> none  [the longest x1 1.59 us: on_device(): lax.fori_loop(0, cut_count + group_count - 1, backward_section, back_state)]
    mul x2 -> x0, other arithmetic: 1.82 us -> none  [the longest x1 1.75 us: fresnel_tables(): far_imag = -sin_table * factor]
    unnamed x8 -> x14, local copies, waits for them, and re-layouts: 1.59 us -> 3.23 us
  transfers between devices with their start and end apart: 6 -> 9, of which waited for: 6 -> 3; matrix products, arithmetic and copies ran while one was open for 9% -> 0% of each run, Pallas kernels for 0% -> 10%
where the time goes in v1:
time: 50.2 us; the launch traced here: 49.8 us
  waiting for transfers between devices  21.4 us (43%)
  starting transfers between devices  15 us (30%)
  Pallas kernels  10 us (20%)
  local copies, waits for them, and re-layouts  3.23 us (6%)
    ppermute x2, waiting for transfers between devices, both(): lax.ppermute(value, 'tile', [(k, (k + steps) % count) for k in range(coun...  14.8 us
    ppermute x7, starting transfers between devices, hop(): return lax.ppermute(value, axes, pairs)  14 us
    ppermute x7, waiting for transfers between devices, hop(): return lax.ppermute(value, axes, pairs)  6.62 us
    unnamed x14, local copies, waits for them, and re-layouts  3.23 us
    pallas_call x1, Pallas kernels, on_device(): call(third_kernel, (shaped((2, W, W), jnp.bfloat16), shaped((2, W, W), jn...  1.99 us
    pallas_call x1, Pallas kernels, on_device(): call(second_kernel, (shaped((2, W, W), jnp.float32), shaped((2, W, W), jn...  1.82 us
    pallas_call x1, Pallas kernels, on_device(): call(first_kernel, shaped((2, W, W), jnp.bfloat16), [SMEM, VMEM, VMEM, VM...  1.79 us
    pallas_call x1, Pallas kernels, on_device(): call(place_kernel, shaped(transmission.shape, jnp.float32), [SMEM, SMEM,...  1.74 us
  transfers between devices with their start and end apart: 9, of which 3 were waited for; matrix products, arithmetic and copies ran while one was open for 0% of the time, Pallas kernels for 10%

profile of v1, /device:TPU:1, one launch (start us, length us, event | category | flops | bytes accessed | tf_op | source)
XLA Modules:
  0.0 49.8 jit_solution(4566474099152079395)
XLA Ops:
  0.0 5.3 %collective-permute-start.4 = (f32[2,256,512]{2,1,0:T(8,128)}, f32[2,256,512]{2,1,0:T(8,128)S(1)}, u32[]{:S(2)}, u32[]{:S(2)}) collective-permute-start(f32[2,256,512]{2,1,0:T(8,128)} %bitcast.2), channel_id=1, source_target_pairs={{128,0},{129,1},{130,2},{131,3},{132,4},{133,5},{134,6},{135,7},{1... | collective-permute-start | bytes 3145736 | tf_op jit(solution)/shard_map/ppermute | solution.py:208
  5.3 0.0 copy-done.6
  5.3 0.0 copy-start
  5.3 1.2 %copy-done = f32[2,1,256,512]{3,2,1,0:T(8,128)S(1)} copy-done((f32[2,1,256,512]{3,2,1,0:T(8,128)S(1)}, f32[2,1,256,512]{3,2,1,0:T(8,128)}, u32[]{:S(2)}) %copy-start) | copy-done | bytes 1048600
  6.5 0.9 %copy-done.5 = f32[1,256,256]{2,1,0:T(8,128)S(1)} copy-done((f32[1,256,256]{2,1,0:T(8,128)S(1)}, f32[1,256,256]{2,1,0:T(8,128)}, u32[]{:S(2)}) %copy-start.5) | copy-done | bytes 262168
  7.5 0.8 %encode.1 = (s16[2,272,256]{2,1,0:T(8,128)(2,1)S(1)}, s16[256,256]{1,0:T(8,128)(2,1)S(1)}) custom-call(s32[1,2]{1,0:T(1,128)S(1)} %copy-done.6, f32[2,1,256,512]{3,2,1,0:T(8,128)S(1)} %copy-done, f32[1,256,256]{2,1,0:T(8,128)S(1)} %copy-done.5), custom_call_target="tpu_custom_call" | custom-call | tf_op jit(solution)/shard_map/encode/pallas_call | solution.py:215
  8.3 0.0 copy-start.2
  8.3 0.8 %collective-permute-start.5 = (s16[2,272,256]{2,1,0:T(8,128)(2,1)S(1)}, s16[2,272,256]{2,1,0:T(8,128)(2,1)S(1)}, u32[]{:S(2)}, u32[]{:S(2)}) collective-permute-start(s16[2,272,256]{2,1,0:T(8,128)(2,1)S(1)} %get-tuple-element.12), channel_id=1, source_target_pairs={{0,1},{1,2},{2,3},{3,4},{4,5},{5,6},{6,7},{7,8},{8,9},{9,10},{10,1... | collective-permute-start | bytes 835592 | tf_op jit(solution)/shard_map/ppermute | solution.py:208
  9.1 3.4 %collective-permute-start.3 = (s16[2,272,256]{2,1,0:T(8,128)(2,1)S(1)}, s16[2,272,256]{2,1,0:T(8,128)(2,1)S(1)}, u32[]{:S(2)}, u32[]{:S(2)}) collective-permute-start(s16[2,272,256]{2,1,0:T(8,128)(2,1)S(1)} %get-tuple-element.12), channel_id=1, source_target_pairs={{128,1},{129,2},{130,3},{131,4},{132,5},{133,6},{134,7},{135,8},{1... | collective-permute-start | bytes 835592 | tf_op jit(solution)/shard_map/ppermute | solution.py:208
  12.4 1.3 %collective-permute-start.2 = (s16[256,256]{1,0:T(8,128)(2,1)S(1)}, s16[256,256]{1,0:T(8,128)(2,1)S(1)}, u32[]{:S(2)}, u32[]{:S(2)}) collective-permute-start(s16[256,256]{1,0:T(8,128)(2,1)S(1)} %get-tuple-element.11), channel_id=1, source_target_pairs={{128,1},{129,2},{130,3},{131,4},{132,5},{133,6},{134,7},{135,8},{1... | collective-permute-start | bytes 393224 | tf_op jit(solution)/shard_map/ppermute | solution.py:208
  13.8 1.0 %collective-permute-start = (s32[1,2]{1,0:T(1,128)S(1)}, s32[1,2]{1,0:T(1,128)S(1)}, u32[]{:S(2)}, u32[]{:S(2)}) collective-permute-start(s32[1,2]{1,0:T(1,128)S(1)} %copy-done.6), channel_id=1, source_target_pairs={{0,1},{1,2},{2,3},{3,4},{4,5},{5,6},{6,7},{7,8},{8,9},{9,10},{10,1... | collective-permute-start | bytes 32 | tf_op jit(solution)/shard_map/ppermute | solution.py:211
  14.7 12.2 %collective-permute-done.offsets.before = s32[1,2]{1,0:T(1,128)S(1)} collective-permute-done((s32[1,2]{1,0:T(1,128)S(1)}, s32[1,2]{1,0:T(1,128)S(1)}, u32[]{:S(2)}, u32[]{:S(2)}) %collective-permute-start) | collective-permute-done | bytes 40 | tf_op jit(solution)/shard_map/ppermute | solution.py:211
  26.9 0.0 collective-permute-start.1
  26.9 1.0 %copy-done.4 = f32[2,256,256]{2,1,0:T(8,128)S(1)} copy-done((f32[2,256,256]{2,1,0:T(8,128)S(1)}, f32[2,256,256]{2,1,0:T(8,128)}, u32[]{:S(2)}) %copy-start.4) | copy-done | bytes 524312
  28.0 0.8 %roll.1.rolled = f32[2,256,256]{2,1,0:T(8,128)S(1)} custom-call(s32[1,2]{1,0:T(1,128)S(1)} %collective-permute-done.offsets.before, f32[2,256,256]{2,1,0:T(8,128)S(1)} %copy-done.4), custom_call_target="tpu_custom_call" | custom-call | tf_op jit(solution)/shard_map/roll/pallas_call | solution.py:225
  28.8 0.0 copy-start.3
  28.8 0.0 collective-permute-done.5.coded
  28.8 1.8 %first.1.psi = bf16[2,256,256]{2,1,0:T(8,128)(2,1)S(1)} custom-call(s32[1,2]{1,0:T(1,128)S(1)} %collective-permute-done.offsets.before, s16[2,272,256]{2,1,0:T(8,128)(2,1)S(1)} %collective-permute-done.5.coded, f32[2,1,256,512]{3,2,1,0:T(8,128)S(1)} %copy-done.1, f32[2,256,256]{2,1,0:T(8,128)S(1)} %roll.1.rolled, bf16[6,256,256]{2,1,0:T(8,128)(2,1)S(1)} %copy-done.2), custom_call_target="tpu_custom_call" | custom-call | tf_op jit(solution)/shard_map/first/pallas_call | solution.py:226
  30.6 0.0 collective-permute-done.3.coded
  30.6 0.0 collective-permute-done.4.other
  30.6 1.8 %second.1 = (f32[2,256,256]{2,1,0:T(8,128)S(1)}, f32[2,256,256]{2,1,0:T(8,128)S(1)}) custom-call(s32[1,2]{1,0:T(1,128)S(1)} %collective-permute-done.offsets.before, s16[2,272,256]{2,1,0:T(8,128)(2,1)S(1)} %collective-permute-done.3.coded, f32[2,256,512]{2,1,0:T(8,128)S(1)} %collective-permute-done.4.other, bf16[2,256,256]{2,1,0:T(8,128)(2,1)S(1)} %first.1.psi, ...), custom_call_target="tpu_custom_call" | custom-call | tf_op jit(solution)/shard_map/second/pallas_call | solution.py:229
  32.5 2.6 %collective-permute-done.1.live = s32[1]{0:T(128)} collective-permute-done((s32[1]{0:T(128)}, s32[1]{0:T(128)}, u32[]{:S(2)}, u32[]{:S(2)}) %collective-permute-start.1) | collective-permute-done | bytes 36 | tf_op jit(solution)/shard_map/ppermute | solution.py:211
  35.0 0.0 collective-permute-done.2.coded_measured
  35.0 2.0 %third.1 = (bf16[2,256,256]{2,1,0:T(8,128)(2,1)S(1)}, bf16[2,256,256]{2,1,0:T(8,128)(2,1)S(1)}) custom-call(s32[1]{0:T(128)} %collective-permute-done.1.live, s16[256,256]{1,0:T(8,128)(2,1)S(1)} %collective-permute-done.2.coded_measured, f32[2,256,256]{2,1,0:T(8,128)S(1)} %get-tuple-element.13.field, bf16[2,256,256]{2,1,0:T(8,128)(2,1)S(1)} %first.1.psi, ...), custom_call_target="tpu_custom_call" | custom-call | tf_op jit(solution)/shard_map/third/pallas_call | solution.py:235
  37.0 1.2 %fourth.1.spill_first = bf16[2,256,256]{2,1,0:T(8,128)(2,1)S(1)} custom-call(bf16[2,256,256]{2,1,0:T(8,128)(2,1)S(1)} %get-tuple-element.15.wave_grad, f32[2,256,256]{2,1,0:T(8,128)S(1)} %roll.1.rolled, bf16[6,256,256]{2,1,0:T(8,128)(2,1)S(1)} %copy-done.2), custom_call_target="tpu_custom_call" | custom-call | tf_op jit(solution)/shard_map/fourth/pallas_call | solution.py:243
  38.2 0.7 %collective-permute-start.6 = (bf16[2,256,256]{2,1,0:T(8,128)(2,1)S(1)}, bf16[2,256,256]{2,1,0:T(8,128)(2,1)S(1)}, u32[]{:S(2)}, u32[]{:S(2)}) collective-permute-start(bf16[2,256,256]{2,1,0:T(8,128)(2,1)S(1)} %fourth.1.spill_first), channel_id=1, source_target_pairs={{0,127},{1,0},{2,1},{3,2},{4,3},{5,4},{6,5},{7,6},{8,7},{9,8},{10,... | collective-permute-start | bytes 786440 | tf_op jit(solution)/shard_map/ppermute | solution.py:208
  38.9 1.3 %collective-permute-start.7 = (bf16[2,256,256]{2,1,0:T(8,128)(2,1)S(1)}, bf16[2,256,256]{2,1,0:T(8,128)(2,1)S(1)}, u32[]{:S(2)}, u32[]{:S(2)}) collective-permute-start(bf16[2,256,256]{2,1,0:T(8,128)(2,1)S(1)} %get-tuple-element.16), channel_id=1, source_target_pairs={{0,255},{1,128},{2,129},{3,130},{4,131},{5,132},{6,133},{7,134},{8... | collective-permute-start | bytes 786440 | tf_op jit(solution)/shard_map/ppermute | solution.py:208
  40.2 1.3 %collective-permute-start.8 = (bf16[2,256,256]{2,1,0:T(8,128)(2,1)S(1)}, bf16[2,256,256]{2,1,0:T(8,128)(2,1)S(1)}, u32[]{:S(2)}, u32[]{:S(2)}) collective-permute-start(bf16[2,256,256]{2,1,0:T(8,128)(2,1)S(1)} %get-tuple-element.16), channel_id=1, source_target_pairs={{0,128},{1,129},{2,130},{3,131},{4,132},{5,133},{6,134},{7,135},{8... | collective-permute-start | bytes 786440 | tf_op jit(solution)/shard_map/ppermute | solution.py:208
  41.5 0.0 collective-permute-done.6.own_first
  41.5 6.6 %collective-permute-done.7.own_second = bf16[2,256,256]{2,1,0:T(8,128)(2,1)S(1)} collective-permute-done((bf16[2,256,256]{2,1,0:T(8,128)(2,1)S(1)}, bf16[2,256,256]{2,1,0:T(8,128)(2,1)S(1)}, u32[]{:S(2)}, u32[]{:S(2)}) %collective-permute-start.7) | collective-permute-done | bytes 262176 | tf_op jit(solution)/shard_map/ppermute | solution.py:208
  48.1 0.0 collective-permute-done.8.spill_second
  48.1 1.7 %place.1 = f32[2,1,256,512]{3,2,1,0:T(8,128)} custom-call(s32[1,2]{1,0:T(1,128)S(1)} %copy-done.6, s32[1,2]{1,0:T(1,128)S(1)} %collective-permute-done.offsets.before, s32[1]{0:T(128)} %bitcast.core, bf16[2,256,256]{2,1,0:T(8,128)(2,1)S(1)} %collective-permute-done.6.own_first, bf16[2,256,256]{2,1,0:T(8,128)(2,1)S(1)} %collective-permute-done.7.own_second, ...), custom_call_target="tpu_custom_call" | custom-call | tf_op jit(solution)/shard_map/place/pallas_call | solution.py:247
  (7 shorter events, 0.0 us)
Async XLA Ops:
  0.0 5.3 %copy-start.6 = (s32[1,2]{1,0:T(1,128)S(1)}, s32[1,2]{1,0:T(1,128)}, u32[]{:S(2)}) copy-start(s32[1,2]{1,0:T(1,128)} %offsets.3) | copy-start | bytes 28
  0.0 30.6 %collective-permute-start.4 = (f32[2,256,512]{2,1,0:T(8,128)}, f32[2,256,512]{2,1,0:T(8,128)S(1)}, u32[]{:S(2)}, u32[]{:S(2)}) collective-permute-start(f32[2,256,512]{2,1,0:T(8,128)} %bitcast.2), channel_id=1, source_target_pairs={{128,0},{129,1},{130,2},{131,3},{132,4},{133,5},{134,6},{135,7},{1... | collective-permute-start | bytes 3145736 | tf_op jit(solution)/shard_map/ppermute | solution.py:208
  5.3 1.2 %copy-start = (f32[2,1,256,512]{3,2,1,0:T(8,128)S(1)}, f32[2,1,256,512]{3,2,1,0:T(8,128)}, u32[]{:S(2)}) copy-start(f32[2,1,256,512]{3,2,1,0:T(8,128)} %own.3) | copy-start | bytes 3145732
  6.5 0.9 %copy-start.5 = (f32[1,256,256]{2,1,0:T(8,128)S(1)}, f32[1,256,256]{2,1,0:T(8,128)}, u32[]{:S(2)}) copy-start(f32[1,256,256]{2,1,0:T(8,128)} %measured.1) | copy-start | bytes 786436
  7.5 21.3 %copy-start.1 = (f32[2,1,256,512]{3,2,1,0:T(8,128)S(1)}, f32[2,1,256,512]{3,2,1,0:T(8,128)}, u32[]{:S(2)}) copy-start(f32[2,1,256,512]{3,2,1,0:T(8,128)} %own.3) | copy-start | bytes 3145732
  8.3 20.5 %copy-start.2 = (bf16[6,256,256]{2,1,0:T(8,128)(2,1)S(1)}, bf16[6,256,256]{2,1,0:T(8,128)(2,1)}, u32[]{:S(2)}) copy-start(bf16[6,256,256]{2,1,0:T(8,128)(2,1)} %constant.10.clone.prop) | copy-start | bytes 2359300
  8.3 20.5 %collective-permute-start.5 = (s16[2,272,256]{2,1,0:T(8,128)(2,1)S(1)}, s16[2,272,256]{2,1,0:T(8,128)(2,1)S(1)}, u32[]{:S(2)}, u32[]{:S(2)}) collective-permute-start(s16[2,272,256]{2,1,0:T(8,128)(2,1)S(1)} %get-tuple-element.12), channel_id=1, source_target_pairs={{0,1},{1,2},{2,3},{3,4},{4,5},{5,6},{6,7},{7,8},{8,9},{9,10},{10,1... | collective-permute-start | bytes 835592 | tf_op jit(solution)/shard_map/ppermute | solution.py:208
  9.1 21.5 %collective-permute-start.3 = (s16[2,272,256]{2,1,0:T(8,128)(2,1)S(1)}, s16[2,272,256]{2,1,0:T(8,128)(2,1)S(1)}, u32[]{:S(2)}, u32[]{:S(2)}) collective-permute-start(s16[2,272,256]{2,1,0:T(8,128)(2,1)S(1)} %get-tuple-element.12), channel_id=1, source_target_pairs={{128,1},{129,2},{130,3},{131,4},{132,5},{133,6},{134,7},{135,8},{1... | collective-permute-start | bytes 835592 | tf_op jit(solution)/shard_map/ppermute | solution.py:208
  12.4 22.6 %collective-permute-start.2 = (s16[256,256]{1,0:T(8,128)(2,1)S(1)}, s16[256,256]{1,0:T(8,128)(2,1)S(1)}, u32[]{:S(2)}, u32[]{:S(2)}) collective-permute-start(s16[256,256]{1,0:T(8,128)(2,1)S(1)} %get-tuple-element.11), channel_id=1, source_target_pairs={{128,1},{129,2},{130,3},{131,4},{132,5},{133,6},{134,7},{135,8},{1... | collective-permute-start | bytes 393224 | tf_op jit(solution)/shard_map/ppermute | solution.py:208
  13.8 13.2 %collective-permute-start = (s32[1,2]{1,0:T(1,128)S(1)}, s32[1,2]{1,0:T(1,128)S(1)}, u32[]{:S(2)}, u32[]{:S(2)}) collective-permute-start(s32[1,2]{1,0:T(1,128)S(1)} %copy-done.6), channel_id=1, source_target_pairs={{0,1},{1,2},{2,3},{3,4},{4,5},{5,6},{6,7},{7,8},{8,9},{9,10},{10,1... | collective-permute-start | bytes 32 | tf_op jit(solution)/shard_map/ppermute | solution.py:211
  26.9 8.1 %collective-permute-start.1 = (s32[1]{0:T(128)}, s32[1]{0:T(128)}, u32[]{:S(2)}, u32[]{:S(2)}) collective-permute-start(s32[1]{0:T(128)} %param.11), channel_id=1, source_target_pairs={{0,1},{1,2},{2,3},{3,4},{4,5},{5,6},{6,7},{7,8},{8,9},{9,10},{10,1... | collective-permute-start | bytes 20 | tf_op jit(solution)/shard_map/ppermute | solution.py:211
  26.9 1.0 %copy-start.4 = (f32[2,256,256]{2,1,0:T(8,128)S(1)}, f32[2,256,256]{2,1,0:T(8,128)}, u32[]{:S(2)}) copy-start(f32[2,256,256]{2,1,0:T(8,128)} %illumination.1) | copy-start | bytes 1572868
  28.8 1.9 %copy-start.3 = (bf16[6,256,256]{2,1,0:T(8,128)(2,1)S(1)}, bf16[6,256,256]{2,1,0:T(8,128)(2,1)}, u32[]{:S(2)}) copy-start(bf16[6,256,256]{2,1,0:T(8,128)(2,1)} %constant.11.clone.far) | copy-start | bytes 2359300
  38.2 3.3 %collective-permute-start.6 = (bf16[2,256,256]{2,1,0:T(8,128)(2,1)S(1)}, bf16[2,256,256]{2,1,0:T(8,128)(2,1)S(1)}, u32[]{:S(2)}, u32[]{:S(2)}) collective-permute-start(bf16[2,256,256]{2,1,0:T(8,128)(2,1)S(1)} %fourth.1.spill_first), channel_id=1, source_target_pairs={{0,127},{1,0},{2,1},{3,2},{4,3},{5,4},{6,5},{7,6},{8,7},{9,8},{10,... | collective-permute-start | bytes 786440 | tf_op jit(solution)/shard_map/ppermute | solution.py:208
  38.9 9.2 %collective-permute-start.7 = (bf16[2,256,256]{2,1,0:T(8,128)(2,1)S(1)}, bf16[2,256,256]{2,1,0:T(8,128)(2,1)S(1)}, u32[]{:S(2)}, u32[]{:S(2)}) collective-permute-start(bf16[2,256,256]{2,1,0:T(8,128)(2,1)S(1)} %get-tuple-element.16), channel_id=1, source_target_pairs={{0,255},{1,128},{2,129},{3,130},{4,131},{5,132},{6,133},{7,134},{8... | collective-permute-start | bytes 786440 | tf_op jit(solution)/shard_map/ppermute | solution.py:208
  40.2 7.9 %collective-permute-start.8 = (bf16[2,256,256]{2,1,0:T(8,128)(2,1)S(1)}, bf16[2,256,256]{2,1,0:T(8,128)(2,1)S(1)}, u32[]{:S(2)}, u32[]{:S(2)}) collective-permute-start(bf16[2,256,256]{2,1,0:T(8,128)(2,1)S(1)} %get-tuple-element.16), channel_id=1, source_target_pairs={{0,128},{1,129},{2,130},{3,131},{4,132},{5,133},{6,134},{7,135},{8... | collective-permute-start | bytes 786440 | tf_op jit(solution)/shard_map/ppermute | solution.py:208

commit v2 on v1

v2 whole, which is shorter than its diff:
```python
import functools
import math

import jax
import jax.numpy as jnp
import numpy as np
from jax import lax
from jax.experimental import pallas as pl
from jax.experimental.pallas import tpu as pltpu
from jax.sharding import PartitionSpec as P


W = 256
HEAD = 16
TOP = 32000.0
STEP = 32
ASIDE = 16
FLUSH = 64
MEASURED_STEP = 5.0 / TOP
VMEM = pl.BlockSpec(memory_space=pltpu.VMEM)
ANY = pl.BlockSpec(memory_space=pl.ANY)
SMEM = pl.BlockSpec(memory_space=pltpu.SMEM)


def split_table(matrix):
    parts = []
    for factor in (matrix.real, matrix.imag - matrix.real, matrix.real + matrix.imag):
        factor = np.asarray(factor, np.float32)
        high = factor.astype(jnp.bfloat16)
        low = (factor - high.astype(np.float32)).astype(jnp.bfloat16)
        parts += [high, low]
    return np.stack(parts)


@functools.lru_cache(None)
def tables():
    freq = np.arange(W)
    signed = np.where(freq < W // 2, freq, freq - W).astype(np.float64)
    phase = np.pi * signed * signed / (4 * W)
    basis = np.exp(2j * np.pi * ((freq[:, None] * freq[None, :]) % W) / W)
    prop = (basis * np.exp(-1j * phase)[None, :]) @ np.conj(basis).T / W
    far = np.conj(basis) / math.sqrt(W)
    return split_table(prop), split_table(far)


def halves(value):
    high = value.astype(jnp.bfloat16)
    low = (value - high.astype(jnp.float32)).astype(jnp.bfloat16)
    return high, low


def dot(first, second):
    return jnp.dot(first, second, preferred_element_type=jnp.float32)


def right(value, table, which):
    high, low = halves(value)
    big, small = table[2 * which], table[2 * which + 1]
    return dot(high, big) + dot(low, big) + dot(high, small)


def left(value, table, which):
    high, low = halves(value)
    big, small = table[2 * which], table[2 * which + 1]
    return dot(big, high) + dot(big, low) + dot(small, high)


def product(times, real, imag, table, conj):
    both = times(real + imag, table, 0)
    if conj:
        return both + times(imag, table, 1), both - times(real, table, 2)
    return both - times(imag, table, 2), both + times(real, table, 1)


def transform(real, imag, table, conj):
    real, imag = product(right, real, imag, table, conj)
    return product(left, real, imag, table, conj)


def iota(dim):
    return lax.broadcasted_iota(jnp.int32, (STEP, W), dim)


def windowed(full, part, rows, col):
    return jnp.where(iota(1) >= col, full[part, rows, :W], full[part, rows, W:])


def encode_kernel(offsets, live, own, coded):
    col = offsets[0, 1]
    held = own.at[:, 0]
    peak = jnp.zeros((8, W), jnp.float32)
    for start in range(0, W, STEP):
        rows = pl.ds(start, STEP)
        real, imag = windowed(held, 0, rows, col), windowed(held, 1, rows, col)
        high = jnp.maximum(jnp.abs(real), jnp.abs(imag))
        for piece in range(0, STEP, 8):
            peak = jnp.maximum(peak, high[piece : piece + 8])
    peak = jnp.max(jnp.max(peak, axis=1, keepdims=True), axis=0, keepdims=True)
    peak = jnp.broadcast_to(jnp.maximum(peak, 1e-30), (1, W))
    power = jnp.ceil(jnp.log(peak) * (1.0 / math.log(2.0)))
    gain = jnp.exp2(-power) * TOP
    for part in range(2):
        for start in range(0, W, STEP):
            rows = pl.ds(start, STEP)
            scaled = jnp.round(windowed(held, part, rows, col) * gain)
            coded[part, rows, :] = scaled.astype(jnp.int32).astype(jnp.int16)
    flag = jnp.where(live[0] > 0, 1, 0)
    coded[0, pl.ds(W, HEAD), :] = jnp.broadcast_to(power.astype(jnp.int32), (HEAD, W)).astype(jnp.int16)
    coded[1, pl.ds(W, HEAD), :] = jnp.full((HEAD, W), flag, jnp.int32).astype(jnp.int16)


def mixed_kernel(before, core, live, own, measured, coded, mixed):
    encode_kernel(before, live, own, coded)

    @pl.when(core[0] == 0)
    def _():
        for start in range(0, W, STEP):
            rows = pl.ds(start, STEP)
            scaled = jnp.round(measured[0, rows, :] * (1.0 / MEASURED_STEP))
            mixed[0, rows, :] = scaled.astype(jnp.int32).astype(jnp.int16)

    @pl.when(core[0] != 0)
    def _():
        mixed[...] = coded[...]


def head_of(coded, part):
    return coded[part, pl.ds(W, HEAD), :].astype(jnp.int32).astype(jnp.float32)[0:1]


def gain_of(coded):
    return jnp.exp2(head_of(coded, 0)) * (1.0 / TOP)


def decoded(coded, part, rows, gain):
    return coded[part, rows, :].astype(jnp.int32).astype(jnp.float32) * gain


def roll_kernel(offsets, before, core, illumination, rolled):
    row = lax.rem(jnp.where(core[0] == 0, before[0, 0], offsets[0, 0]), W)
    col = lax.rem(jnp.where(core[0] == 0, before[0, 1], offsets[0, 1]), W)
    for part in range(2):
        rolled[part] = pltpu.roll(pltpu.roll(illumination[part], row, 0), col, 1)


def times_patch(wave, patch, out):
    for start in range(0, W, STEP):
        rows = pl.ds(start, STEP)
        wave_real, wave_imag = wave[0, rows, :].astype(jnp.float32), wave[1, rows, :].astype(jnp.float32)
        patch_real, patch_imag = patch(0, rows, start), patch(1, rows, start)
        out[0, rows, :] = wave_real * patch_real - wave_imag * patch_imag
        out[1, rows, :] = wave_real * patch_imag + wave_imag * patch_real


def chosen(row, upper, lower):
    return lambda part, rows, start: jnp.where(
        start + iota(0) >= row, lower(part, rows), upper(part, rows)
    )


def first_slice(rolled, patch, prop, psi, chi):
    times_patch(rolled, patch, chi)
    out_real, out_imag = transform(chi[0], chi[1], prop, False)
    psi[0] = out_real.astype(jnp.bfloat16)
    psi[1] = out_imag.astype(jnp.bfloat16)


def first_kernel(offsets, before, core, direct, own, rolled, prop, psi, chi):
    @pl.when(core[0] == 0)
    def _():
        gain = gain_of(direct)
        local = own.at[:, 0]
        patch = chosen(
            before[0, 0],
            lambda part, rows: windowed(local, part, rows, before[0, 1]),
            lambda part, rows: decoded(direct, part, rows, gain),
        )
        first_slice(rolled, patch, prop, psi, chi)


def keeping(given, patch):
    def kept(part, rows, start):
        value = given(part, rows, start)
        patch[part, rows, :] = value
        return value

    return kept


def second_slice(given, psi, far, patch, field, chi):
    times_patch(psi, keeping(given, patch), chi)
    out_real, out_imag = transform(chi[0], chi[1], far, False)
    field[0] = out_real
    field[1] = out_imag


def second_kernel(offsets, before, core, crossed, edge, rolled, early, prop, far, psi, patch, field, chi):
    row = jnp.where(core[0] == 0, before[0, 0], offsets[0, 0])
    gain_crossed, gain_edge = gain_of(crossed), gain_of(edge)
    given = chosen(
        row,
        lambda part, rows: decoded(edge, part, rows, gain_edge),
        lambda part, rows: decoded(crossed, part, rows, gain_crossed),
    )

    @pl.when(core[0] == 0)
    def _():
        psi[...] = early[...]
        second_slice(given, psi, far, patch, field, chi)

    @pl.when(core[0] != 0)
    def _():
        first_slice(rolled, given, prop, psi, chi)


def late_kernel(offsets, core, border, own, psi, far, patch, field, chi):
    @pl.when(core[0] != 0)
    def _():
        gain_border = gain_of(border)
        local = own.at[:, 0]
        last = chosen(
            offsets[0, 0],
            lambda part, rows: decoded(border, part, rows, gain_border),
            lambda part, rows: windowed(local, part, rows, offsets[0, 1]),
        )
        second_slice(last, psi, far, patch, field, chi)


def conj_times(first, real, imag, out):
    for start in range(0, W, STEP):
        rows = pl.ds(start, STEP)
        keep = slice(start, start + STEP)
        first_real, first_imag = first[0, rows, :].astype(jnp.float32), first[1, rows, :].astype(jnp.float32)
        out[0, rows, :] = (first_real * real[keep] + first_imag * imag[keep]).astype(out.dtype)
        out[1, rows, :] = (first_real * imag[keep] - first_imag * real[keep]).astype(out.dtype)


def third_kernel(
    core, live, direct, border, measured, field, late_field, psi, patch, late_patch, rolled, prop, far, send, stay, chi, half
):
    def residue(field, target, alive):
        for start in range(0, W, STEP):
            rows = pl.ds(start, STEP)
            real, imag = field[0, rows, :], field[1, rows, :]
            weight = (real * real + imag * imag - target(rows)) * alive
            chi[0, rows, :] = weight * real
            chi[1, rows, :] = weight * imag

    @pl.when(core[0] == 0)
    def _():
        head = head_of(direct, 1)
        residue(field, lambda rows: border[0, rows, :].astype(jnp.int32).astype(jnp.float32) * MEASURED_STEP, head)

    @pl.when(core[0] != 0)
    def _():
        residue(late_field, lambda rows: measured[0, rows, :], jnp.where(live[0] > 0, 1.0, 0.0))

    real, imag = transform(chi[0], chi[1], far, True)

    @pl.when(core[0] == 0)
    def _():
        conj_times(patch, real, imag, half)
        conj_times(psi, real, imag, send)

    @pl.when(core[0] != 0)
    def _():
        conj_times(late_patch, real, imag, half)
        conj_times(psi, real, imag, stay)

    real, imag = transform(half[0].astype(jnp.float32), half[1].astype(jnp.float32), prop, True)

    @pl.when(core[0] == 0)
    def _():
        conj_times(rolled, real, imag, stay)

    @pl.when(core[0] != 0)
    def _():
        conj_times(rolled, real, imag, send)


def place_kernel(offsets, before, core, stay, came, out, staged, sems):
    row, col = offsets[0, 0], offsets[0, 1]
    row_before, col_before = before[0, 0], before[0, 1]

    def place(own, spill):
        copies = []
        for index, start in enumerate(range(0, W, FLUSH)):
            for inner in range(start, start + FLUSH, STEP):
                rows = pl.ds(inner, STEP)
                for part in range(2):
                    mine = jnp.where(inner + iota(0) >= row, own[part, rows, :].astype(jnp.float32), 0.0)
                    theirs = jnp.where(inner + iota(0) < row_before, spill[part, rows, :].astype(jnp.float32), 0.0)
                    here, there = iota(1) >= col, iota(1) >= col_before
                    staged[part, 0, rows, :W] = jnp.where(here, mine, 0.0) + jnp.where(there, theirs, 0.0)
                    staged[part, 0, rows, W:] = jnp.where(here, 0.0, mine) + jnp.where(there, 0.0, theirs)
            block = (slice(None), slice(None), pl.ds(start, FLUSH))
            copies.append(pltpu.make_async_copy(staged.at[block], out.at[block], sems.at[index]))
            copies[-1].start()
        for copy in copies:
            copy.wait()

    @pl.when(core[0] == 0)
    def _():
        place(came, stay)

    @pl.when(core[0] != 0)
    def _():
        place(stay, came)


def call(kernel, outs, specs, scratch=(), out_spec=VMEM, mib=16):
    return pl.pallas_call(
        kernel,
        out_shape=outs,
        in_specs=[{"s": SMEM, "v": VMEM, "a": ANY}[s] for s in specs],
        out_specs=jax.tree.map(lambda _: out_spec, outs),
        scratch_shapes=scratch,
        compiler_params=pltpu.CompilerParams(vmem_limit_bytes=mib << 20),
    )


def shaped(shape, dtype):
    return jax.ShapeDtypeStruct(shape, dtype)


WAVE = shaped((2, W, W), jnp.float32)
HALF_WAVE = shaped((2, W, W), jnp.bfloat16)
CODED = shaped((2, W + HEAD, W), jnp.int16)
CHI = pltpu.VMEM((2, W, W), jnp.float32)


def on_device(transmission, illumination, measured, offsets, live_count):
    prop, far = (jnp.asarray(t) for t in tables())
    count = lax.axis_size("tile")
    core = lax.axis_index("cuts").astype(jnp.int32)[None]

    def permute(value, target):
        pairs = []
        for c in range(2):
            for k in range(count):
                to_core, to_tile = target(c, k)
                pairs.append((c * count + k, to_core * count + to_tile % count))
        return lax.ppermute(value, ("cuts", "tile"), pairs)

    before = permute(offsets, lambda c, k: (c, k + 1))
    place = (offsets, before, core)
    encode = call(encode_kernel, CODED, "ssv")
    ahead = encode(offsets, live_count, transmission)
    direct = permute(ahead, lambda c, k: (0, k + 1) if c == 0 else (1, k - ASIDE))
    behind, mixed = call(mixed_kernel, (CODED, CODED), "sssvv")(before, core, live_count, transmission, measured)
    crossed = permute(ahead, lambda c, k: (1, k) if c == 0 else (0, k + 1))
    border = permute(mixed, lambda c, k: (0, k + 1) if c == 0 else (1, k - 1))
    edge = permute(behind, lambda c, k: (1, k - 1) if c == 0 else (0, k))
    rolled = call(roll_kernel, WAVE, "sssv")(*place, illumination)
    early = call(first_kernel, HALF_WAVE, "sssvvvv", [CHI])(*place, direct, transmission, rolled, prop)
    psi, patch, field = call(second_kernel, (HALF_WAVE, WAVE, WAVE), "sss" + "v" * 6, [CHI])(
        *place, crossed, edge, rolled, early, prop, far
    )
    late_patch, late_field = call(late_kernel, (WAVE, WAVE), "ssvvvv", [CHI])(
        offsets, core, border, transmission, psi, far
    )
    send, stay = call(
        third_kernel, (HALF_WAVE, HALF_WAVE), "ss" + "v" * 11, [CHI, pltpu.VMEM((2, W, W), jnp.bfloat16)]
    )(core, live_count, direct, border, measured, field, late_field, psi, patch, late_patch, rolled, prop, far)
    came = permute(send, lambda c, k: (1 - c, k))
    return call(
        place_kernel,
        shaped(transmission.shape, jnp.float32),
        "sssvv",
        [pltpu.VMEM(transmission.shape, jnp.float32), pltpu.SemaphoreType.DMA((W // FLUSH,))],
        ANY,
    )(*place, stay, came)


def solution(mesh):
    placed = (P(None, "cuts", "tile", None), P(), P("tile", None, None), P("tile", None), P("tile"))
    return jax.shard_map(
        on_device,
        mesh=mesh,
        in_specs=placed,
        out_specs=P(None, "cuts", "tile", None),
        check_vma=False,
    )
```

time: 50.2 us -> 36.3 us (0.72)
  waiting for transfers between devices: 21.4 us -> 3.92 us
  starting transfers between devices: 15 us -> 19.5 us
  local copies, waits for them, and re-layouts: 3.23 us -> 1.25 us
  Pallas kernels: 10 us -> 10.8 us
  between operations: 0.2 us -> 0.78 us
    ppermute x9 -> x6, waiting for transfers between devices: 21.4 us -> 3.92 us  [permute(): return lax.ppermute(value, ('cuts', 'tile'), pairs)]
    ppermute x9 -> x6, starting transfers between devices: 15 us -> 19.5 us  [permute(): return lax.ppermute(value, ('cuts', 'tile'), pairs)]
    unnamed x14, local copies, waits for them, and re-layouts: 3.23 us -> 1.25 us
    pallas_call x7 -> x8, Pallas kernels: 10 us -> 10.8 us  [the longest x1 2.63 us: on_device(): call(third_kernel, (HALF_WAVE, HALF_WAVE), 'ss' + 'v' * 11, [CHI, pltpu.V...]
  transfers between devices with their start and end apart: 9 -> 6, of which waited for: 3 -> 3; matrix products, arithmetic and copies ran while one was open for 0% -> 0% of each run, Pallas kernels for 10% -> 13%
where the time goes in v2:
time: 36.3 us; the launch traced here: 36.2 us
  starting transfers between devices  19.5 us (54%)
  Pallas kernels  10.8 us (30%)
  waiting for transfers between devices  3.92 us (11%)
  local copies, waits for them, and re-layouts  1.25 us (3%)
  between operations  0.78 us (2%)
    ppermute x6, starting transfers between devices, permute(): return lax.ppermute(value, ('cuts', 'tile'), pairs)  19.5 us
    ppermute x6, waiting for transfers between devices, permute(): return lax.ppermute(value, ('cuts', 'tile'), pairs)  3.92 us
    pallas_call x1, Pallas kernels, on_device(): call(third_kernel, (HALF_WAVE, HALF_WAVE), 'ss' + 'v' * 11, [CHI, pltpu.V...  2.63 us
    pallas_call x1, Pallas kernels, on_device(): call(late_kernel, (WAVE, WAVE), 'ssvvvv', [CHI])  1.86 us
    pallas_call x1, Pallas kernels, on_device(): call(second_kernel, (HALF_WAVE, WAVE, WAVE), 'sss' + 'v' * 6, [CHI])  1.84 us
    pallas_call x1, Pallas kernels, on_device(): call(place_kernel, shaped(transmission.shape, jnp.float32), 'sssvv', [plt...  1.6 us
    unnamed x14, local copies, waits for them, and re-layouts  1.25 us
    pallas_call x1, Pallas kernels, on_device(): rolled = call(roll_kernel, WAVE, 'sssv')(*place, illumination)  0.78 us
  transfers between devices with their start and end apart: 6, of which 3 were waited for; matrix products, arithmetic and copies ran while one was open for 0% of the time, Pallas kernels for 13%

profile of v2, /device:TPU:1, one launch (start us, length us, event | category | flops | bytes accessed | tf_op | source)
XLA Modules:
  0.0 36.2 jit_solution(891696784126731554)
XLA Ops:
  0.0 0.0 copy-start.6
  0.0 2.0 %collective-permute-start = (s32[1,2]{1,0:T(1,128)}, s32[1,2]{1,0:T(1,128)S(1)}, u32[]{:S(2)}, u32[]{:S(2)}) collective-permute-start(s32[1,2]{1,0:T(1,128)} %offsets.11), channel_id=1, source_target_pairs={{0,1},{1,2},{2,3},{3,4},{4,5},{5,6},{6,7},{7,8},{8,9},{9,10},{10,1... | collective-permute-start | bytes 32 | tf_op jit(solution)/shard_map/ppermute | solution.py:343
  2.7 0.0 copy-done.6
  2.7 0.0 copy-start
  2.7 1.2 %copy-done = f32[2,1,256,512]{3,2,1,0:T(8,128)S(1)} copy-done((f32[2,1,256,512]{3,2,1,0:T(8,128)S(1)}, f32[2,1,256,512]{3,2,1,0:T(8,128)}, u32[]{:S(2)}) %copy-start) | copy-done | bytes 1048600
  3.9 0.7 %shard_map.73 = s16[2,272,256]{2,1,0:T(8,128)(2,1)S(1)} custom-call(s32[1,2]{1,0:T(1,128)S(1)} %copy-done.6, s32[1]{0:T(128)S(6)} %copy.8.live, f32[2,1,256,512]{3,2,1,0:T(8,128)S(1)} %copy-done), custom_call_target="tpu_custom_call" | custom-call | tf_op jit(solution)/shard_map/pallas_call | solution.py:348
  4.7 2.1 %collective-permute-start.3 = (s16[2,272,256]{2,1,0:T(8,128)(2,1)S(1)}, s16[2,272,256]{2,1,0:T(8,128)(2,1)S(1)}, u32[]{:S(2)}, u32[]{:S(2)}) collective-permute-start(s16[2,272,256]{2,1,0:T(8,128)(2,1)S(1)} %shard_map.73), channel_id=1, source_target_pairs={{0,128},{1,129},{2,130},{3,131},{4,132},{5,133},{6,134},{7,135},{8... | collective-permute-start | bytes 835592 | tf_op jit(solution)/shard_map/ppermute | solution.py:343
  6.8 5.6 %collective-permute-start.1 = (s16[2,272,256]{2,1,0:T(8,128)(2,1)S(1)}, s16[2,272,256]{2,1,0:T(8,128)(2,1)S(1)}, u32[]{:S(2)}, u32[]{:S(2)}) collective-permute-start(s16[2,272,256]{2,1,0:T(8,128)(2,1)S(1)} %shard_map.73), channel_id=1, source_target_pairs={{0,1},{1,2},{2,3},{3,4},{4,5},{5,6},{6,7},{7,8},{8,9},{9,10},{10,1... | collective-permute-start | bytes 835592 | tf_op jit(solution)/shard_map/ppermute | solution.py:343
  12.4 0.0 collective-permute-done.before
  12.4 0.0 copy-done.1
  12.4 0.0 copy-done.4
  12.4 0.0 copy-start.5
  12.4 0.8 %shard_map.74 = (s16[2,272,256]{2,1,0:T(8,128)(2,1)S(1)}, s16[2,272,256]{2,1,0:T(8,128)(2,1)S(1)}) custom-call(s32[1,2]{1,0:T(1,128)S(1)} %collective-permute-done.before, s32[1]{0:T(128)} %bitcast.core, s32[1]{0:T(128)S(6)} %copy.8.live, f32[2,1,256,512]{3,2,1,0:T(8,128)S(1)} %copy-done.1, f32[1,256,256]{2,1,0:T(8,128)S(1)} %copy-done.4), custom_call_target="tpu_custom_call" | custom-call | tf_op jit(solution)/shard_map/pallas_call | solution.py:350
  13.2 0.0 copy-start.2
  13.2 1.4 %collective-permute-start.4 = (s16[2,272,256]{2,1,0:T(8,128)(2,1)S(1)}, s16[2,272,256]{2,1,0:T(8,128)(2,1)S(1)}, u32[]{:S(2)}, u32[]{:S(2)}) collective-permute-start(s16[2,272,256]{2,1,0:T(8,128)(2,1)S(1)} %get-tuple-element.15), channel_id=1, source_target_pairs={{0,255},{1,128},{2,129},{3,130},{4,131},{5,132},{6,133},{7,134},{8... | collective-permute-start | bytes 835592 | tf_op jit(solution)/shard_map/ppermute | solution.py:343
  14.6 3.2 %collective-permute-start.2 = (s16[2,272,256]{2,1,0:T(8,128)(2,1)S(1)}, s16[2,272,256]{2,1,0:T(8,128)(2,1)S(1)}, u32[]{:S(2)}, u32[]{:S(2)}) collective-permute-start(s16[2,272,256]{2,1,0:T(8,128)(2,1)S(1)} %get-tuple-element.14), channel_id=1, source_target_pairs={{0,1},{1,2},{2,3},{3,4},{4,5},{5,6},{6,7},{7,8},{8,9},{9,10},{10,1... | collective-permute-start | bytes 835592 | tf_op jit(solution)/shard_map/ppermute | solution.py:343
  17.8 0.0 copy-done.5
  17.8 0.8 %shard_map.75.rolled = f32[2,256,256]{2,1,0:T(8,128)S(1)} custom-call(s32[1,2]{1,0:T(1,128)S(1)} %copy-done.6, s32[1,2]{1,0:T(1,128)S(1)} %collective-permute-done.before, s32[1]{0:T(128)} %bitcast.core, f32[2,256,256]{2,1,0:T(8,128)S(1)} %copy-done.5), custom_call_target="tpu_custom_call" | custom-call | tf_op jit(solution)/shard_map/pallas_call | solution.py:354
  18.6 0.0 copy-start.3
  18.6 0.0 collective-permute-done.1.direct
  18.6 0.0 copy-done.2
  18.6 0.6 %shard_map.76.early = bf16[2,256,256]{2,1,0:T(8,128)(2,1)S(1)} custom-call(s32[1,2]{1,0:T(1,128)S(1)} %copy-done.6, s32[1,2]{1,0:T(1,128)S(1)} %collective-permute-done.before, s32[1]{0:T(128)} %bitcast.core, s16[2,272,256]{2,1,0:T(8,128)(2,1)S(1)} %collective-permute-done.1.direct, f32[2,1,256,512]{3,2,1,0:T(8,128)S(1)} %copy-done.1, ...), custom_call_target="tpu_custom_call" | custom-call | tf_op jit(solution)/shard_map/pallas_call | solution.py:355
  19.2 0.0 collective-permute-done.3.crossed
  19.2 2.2 %collective-permute-done.4.edge = s16[2,272,256]{2,1,0:T(8,128)(2,1)S(1)} collective-permute-done((s16[2,272,256]{2,1,0:T(8,128)(2,1)S(1)}, s16[2,272,256]{2,1,0:T(8,128)(2,1)S(1)}, u32[]{:S(2)}, u32[]{:S(2)}) %collective-permute-start.4) | collective-permute-done | bytes 278560 | tf_op jit(solution)/shard_map/ppermute | solution.py:343
  21.4 0.0 copy-done.3
  21.4 1.8 %shard_map.77 = (bf16[2,256,256]{2,1,0:T(8,128)(2,1)S(1)}, f32[2,256,256]{2,1,0:T(8,128)S(1)}, f32[2,256,256]{2,1,0:T(8,128)S(1)}) custom-call(s32[1,2]{1,0:T(1,128)S(1)} %copy-done.6, s32[1,2]{1,0:T(1,128)S(1)} %collective-permute-done.before, s32[1]{0:T(128)} %bitcast.core, s16[2,272,256]{2,1,0:T(8,128)(2,1)S(1)} %collective-permute-done.3.crossed, ...), custom_call_target="tpu_custom_call" | custom-call | tf_op jit(solution)/shard_map/pallas_call | solution.py:356
  23.3 0.5 %collective-permute-done.2.border = s16[2,272,256]{2,1,0:T(8,128)(2,1)S(1)} collective-permute-done((s16[2,272,256]{2,1,0:T(8,128)(2,1)S(1)}, s16[2,272,256]{2,1,0:T(8,128)(2,1)S(1)}, u32[]{:S(2)}, u32[]{:S(2)}) %collective-permute-start.2) | collective-permute-done | bytes 278560 | tf_op jit(solution)/shard_map/ppermute | solution.py:343
  23.8 1.9 %shard_map.78 = (f32[2,256,256]{2,1,0:T(8,128)S(1)}, f32[2,256,256]{2,1,0:T(8,128)S(1)}) custom-call(s32[1,2]{1,0:T(1,128)S(1)} %copy-done.6, s32[1]{0:T(128)} %bitcast.core, s16[2,272,256]{2,1,0:T(8,128)(2,1)S(1)} %collective-permute-done.2.border, f32[2,1,256,512]{3,2,1,0:T(8,128)S(1)} %copy-done.1, bf16[2,256,256]{2,1,0:T(8,128)(2,1)S(1)} %get-tuple-element.17.psi, ...), custom_call_target="tpu_custom_call" | custom-call | tf_op jit(solution)/shard_map/pallas_call | solution.py:359
  25.7 2.6 %shard_map.79 = (bf16[2,256,256]{2,1,0:T(8,128)(2,1)S(1)}, bf16[2,256,256]{2,1,0:T(8,128)(2,1)S(1)}) custom-call(s32[1]{0:T(128)} %bitcast.core, s32[1]{0:T(128)S(6)} %copy.8.live, s16[2,272,256]{2,1,0:T(8,128)(2,1)S(1)} %collective-permute-done.1.direct, s16[2,272,256]{2,1,0:T(8,128)(2,1)S(1)} %collective-permute-done.2.border, ...), custom_call_target="tpu_custom_call" | custom-call | tf_op jit(solution)/shard_map/pallas_call | solution.py:362
  28.3 5.1 %collective-permute-start.5 = (bf16[2,256,256]{2,1,0:T(8,128)(2,1)S(1)}, bf16[2,256,256]{2,1,0:T(8,128)(2,1)S(1)}, u32[]{:S(2)}, u32[]{:S(2)}) collective-permute-start(bf16[2,256,256]{2,1,0:T(8,128)(2,1)S(1)} %get-tuple-element.22), channel_id=1, source_target_pairs={{0,128},{1,129},{2,130},{3,131},{4,132},{5,133},{6,134},{7,135},{8... | collective-permute-start | bytes 786440 | tf_op jit(solution)/shard_map/ppermute | solution.py:343
  33.4 1.2 %collective-permute-done.5.came = bf16[2,256,256]{2,1,0:T(8,128)(2,1)S(1)} collective-permute-done((bf16[2,256,256]{2,1,0:T(8,128)(2,1)S(1)}, bf16[2,256,256]{2,1,0:T(8,128)(2,1)S(1)}, u32[]{:S(2)}, u32[]{:S(2)}) %collective-permute-start.5) | collective-permute-done | bytes 262176 | tf_op jit(solution)/shard_map/ppermute | solution.py:343
  34.6 1.6 %shard_map.80 = f32[2,1,256,512]{3,2,1,0:T(8,128)} custom-call(s32[1,2]{1,0:T(1,128)S(1)} %copy-done.6, s32[1,2]{1,0:T(1,128)S(1)} %collective-permute-done.before, s32[1]{0:T(128)} %bitcast.core, bf16[2,256,256]{2,1,0:T(8,128)(2,1)S(1)} %get-tuple-element.21.stay, bf16[2,256,256]{2,1,0:T(8,128)(2,1)S(1)} %collective-permute-done.5.came), custom_call_target="tpu_custom_call" | custom-call | tf_op jit(solution)/shard_map/pallas_call | solution.py:366
  (2 shorter events, 0.0 us)
Async XLA Ops:
  0.0 2.7 %copy-start.6 = (s32[1,2]{1,0:T(1,128)S(1)}, s32[1,2]{1,0:T(1,128)}, u32[]{:S(2)}) copy-start(s32[1,2]{1,0:T(1,128)} %offsets.11) | copy-start | bytes 28
  0.0 12.4 %collective-permute-start = (s32[1,2]{1,0:T(1,128)}, s32[1,2]{1,0:T(1,128)S(1)}, u32[]{:S(2)}, u32[]{:S(2)}) collective-permute-start(s32[1,2]{1,0:T(1,128)} %offsets.11), channel_id=1, source_target_pairs={{0,1},{1,2},{2,3},{3,4},{4,5},{5,6},{6,7},{7,8},{8,9},{9,10},{10,1... | collective-permute-start | bytes 32 | tf_op jit(solution)/shard_map/ppermute | solution.py:343
  2.7 1.2 %copy-start = (f32[2,1,256,512]{3,2,1,0:T(8,128)S(1)}, f32[2,1,256,512]{3,2,1,0:T(8,128)}, u32[]{:S(2)}) copy-start(f32[2,1,256,512]{3,2,1,0:T(8,128)} %own.7) | copy-start | bytes 3145732
  3.9 8.5 %copy-start.1 = (f32[2,1,256,512]{3,2,1,0:T(8,128)S(1)}, f32[2,1,256,512]{3,2,1,0:T(8,128)}, u32[]{:S(2)}) copy-start(f32[2,1,256,512]{3,2,1,0:T(8,128)} %own.7) | copy-start | bytes 3145732
  3.9 8.5 %copy-start.4 = (f32[1,256,256]{2,1,0:T(8,128)S(1)}, f32[1,256,256]{2,1,0:T(8,128)}, u32[]{:S(2)}) copy-start(f32[1,256,256]{2,1,0:T(8,128)} %measured.3) | copy-start | bytes 786436
  4.7 14.5 %collective-permute-start.3 = (s16[2,272,256]{2,1,0:T(8,128)(2,1)S(1)}, s16[2,272,256]{2,1,0:T(8,128)(2,1)S(1)}, u32[]{:S(2)}, u32[]{:S(2)}) collective-permute-start(s16[2,272,256]{2,1,0:T(8,128)(2,1)S(1)} %shard_map.73), channel_id=1, source_target_pairs={{0,128},{1,129},{2,130},{3,131},{4,132},{5,133},{6,134},{7,135},{8... | collective-permute-start | bytes 835592 | tf_op jit(solution)/shard_map/ppermute | solution.py:343
  6.8 11.8 %collective-permute-start.1 = (s16[2,272,256]{2,1,0:T(8,128)(2,1)S(1)}, s16[2,272,256]{2,1,0:T(8,128)(2,1)S(1)}, u32[]{:S(2)}, u32[]{:S(2)}) collective-permute-start(s16[2,272,256]{2,1,0:T(8,128)(2,1)S(1)} %shard_map.73), channel_id=1, source_target_pairs={{0,1},{1,2},{2,3},{3,4},{4,5},{5,6},{6,7},{7,8},{8,9},{9,10},{10,1... | collective-permute-start | bytes 835592 | tf_op jit(solution)/shard_map/ppermute | solution.py:343
  12.4 5.4 %copy-start.5 = (f32[2,256,256]{2,1,0:T(8,128)S(1)}, f32[2,256,256]{2,1,0:T(8,128)}, u32[]{:S(2)}) copy-start(f32[2,256,256]{2,1,0:T(8,128)} %illumination.1) | copy-start | bytes 1572868
  13.2 5.5 %copy-start.2 = (bf16[6,256,256]{2,1,0:T(8,128)(2,1)S(1)}, bf16[6,256,256]{2,1,0:T(8,128)(2,1)}, u32[]{:S(2)}) copy-start(bf16[6,256,256]{2,1,0:T(8,128)(2,1)} %constant.10.clone.prop) | copy-start | bytes 2359300
  13.2 8.2 %collective-permute-start.4 = (s16[2,272,256]{2,1,0:T(8,128)(2,1)S(1)}, s16[2,272,256]{2,1,0:T(8,128)(2,1)S(1)}, u32[]{:S(2)}, u32[]{:S(2)}) collective-permute-start(s16[2,272,256]{2,1,0:T(8,128)(2,1)S(1)} %get-tuple-element.15), channel_id=1, source_target_pairs={{0,255},{1,128},{2,129},{3,130},{4,131},{5,132},{6,133},{7,134},{8... | collective-permute-start | bytes 835592 | tf_op jit(solution)/shard_map/ppermute | solution.py:343
  14.6 9.2 %collective-permute-start.2 = (s16[2,272,256]{2,1,0:T(8,128)(2,1)S(1)}, s16[2,272,256]{2,1,0:T(8,128)(2,1)S(1)}, u32[]{:S(2)}, u32[]{:S(2)}) collective-permute-start(s16[2,272,256]{2,1,0:T(8,128)(2,1)S(1)} %get-tuple-element.14), channel_id=1, source_target_pairs={{0,1},{1,2},{2,3},{3,4},{4,5},{5,6},{6,7},{7,8},{8,9},{9,10},{10,1... | collective-permute-start | bytes 835592 | tf_op jit(solution)/shard_map/ppermute | solution.py:343
  18.6 2.8 %copy-start.3 = (bf16[6,256,256]{2,1,0:T(8,128)(2,1)S(1)}, bf16[6,256,256]{2,1,0:T(8,128)(2,1)}, u32[]{:S(2)}) copy-start(bf16[6,256,256]{2,1,0:T(8,128)(2,1)} %constant.11.clone.far) | copy-start | bytes 2359300
  28.3 6.2 %collective-permute-start.5 = (bf16[2,256,256]{2,1,0:T(8,128)(2,1)S(1)}, bf16[2,256,256]{2,1,0:T(8,128)(2,1)S(1)}, u32[]{:S(2)}, u32[]{:S(2)}) collective-permute-start(bf16[2,256,256]{2,1,0:T(8,128)(2,1)S(1)} %get-tuple-element.22), channel_id=1, source_target_pairs={{0,128},{1,129},{2,130},{3,131},{4,132},{5,133},{6,134},{7,135},{8... | collective-permute-start | bytes 786440 | tf_op jit(solution)/shard_map/ppermute | solution.py:343

commit v3 on v2

--- a/solution.py
+++ b/solution.py
@@ -11,11 +11,13 @@
 
 
 W = 256
+H = W // 2
 HEAD = 16
 TOP = 32000.0
 STEP = 32
 ASIDE = 16
 FLUSH = 64
+LAST_PASSES = 1
 MEASURED_STEP = 5.0 / TOP
 VMEM = pl.BlockSpec(memory_space=pltpu.VMEM)
 ANY = pl.BlockSpec(memory_space=pl.ANY)
@@ -32,6 +34,15 @@
     return np.stack(parts)
 
 
+def embedded(matrix):
+    real = np.block([[matrix.real, -matrix.imag], [matrix.imag, matrix.real]]).astype(np.float32)
+    parts = []
+    for value in (real, real.T):
+        high = value.astype(jnp.bfloat16)
+        parts += [high, (value - high.astype(np.float32)).astype(jnp.bfloat16)]
+    return parts
+
+
 @functools.lru_cache(None)
 def tables():
     freq = np.arange(W)
@@ -40,7 +51,8 @@
     basis = np.exp(2j * np.pi * ((freq[:, None] * freq[None, :]) % W) / W)
     prop = (basis * np.exp(-1j * phase)[None, :]) @ np.conj(basis).T / W
     far = np.conj(basis) / math.sqrt(W)
-    return split_table(prop), split_table(far)
+    same, cross = prop[:H, :H], prop[:H, H:]
+    return np.stack(embedded((same + cross) / 2) + embedded((same - cross) / 2)), split_table(far)
 
 
 def halves(value):
@@ -77,6 +89,59 @@
     return product(left, real, imag, table, conj)
 
 
+def set_parts(ops, which, rows, cols, value, passes):
+    high = value.astype(jnp.bfloat16)
+    ops[2 * which, rows, cols] = high
+    if passes > 1:
+        ops[2 * which + 1, rows, cols] = (value - high.astype(jnp.float32)).astype(jnp.bfloat16)
+
+
+def circulant_dots(ops, prop, acc, side, passes):
+    for which in range(2):
+        high, low = ops[2 * which], ops[2 * which + 1]
+        table = 4 * which + (2 if side == "right" else 0)
+        big, small = prop[table], prop[table + 1]
+        if side == "right":
+            acc[which] = dot(high, big) + dot(low, big) + dot(high, small) if passes > 1 else dot(high, big)
+        else:
+            acc[which] = dot(big, high) + dot(big, low) + dot(small, high) if passes > 1 else dot(big, high)
+
+
+def propagate(given, prop, ops, acc, passes, conj):
+    sign = -1.0 if conj else 1.0
+    left_half, right_half = pl.ds(0, H), pl.ds(H, H)
+    for start in range(0, W, STEP):
+        rows = pl.ds(start, STEP)
+        real, imag = given(rows, start)
+        for value, cols in ((real, left_half), (sign * imag if conj else imag, right_half)):
+            set_parts(ops, 0, rows, cols, value[:, :H] + value[:, H:], passes)
+            set_parts(ops, 1, rows, cols, value[:, :H] - value[:, H:], passes)
+    circulant_dots(ops, prop, acc, "right", passes)
+    for start in range(0, H, STEP):
+        upper, lower = pl.ds(start, STEP), pl.ds(H + start, STEP)
+        for source, target in ((left_half, upper), (right_half, lower)):
+            plus_upper, minus_upper = acc[0, upper, source], acc[1, upper, source]
+            plus_lower, minus_lower = acc[0, lower, source], acc[1, lower, source]
+            for cols, top, bottom in (
+                (left_half, plus_upper + minus_upper, plus_lower + minus_lower),
+                (right_half, plus_upper - minus_upper, plus_lower - minus_lower),
+            ):
+                set_parts(ops, 0, target, cols, top + bottom, passes)
+                set_parts(ops, 1, target, cols, top - bottom, passes)
+    circulant_dots(ops, prop, acc, "left", passes)
+
+
+def propagated(acc, start, conj):
+    inner = start % H
+    real, imag = (
+        acc[0, pl.ds(row, STEP), :] + acc[1, pl.ds(row, STEP), :]
+        if start < H
+        else acc[0, pl.ds(row, STEP), :] - acc[1, pl.ds(row, STEP), :]
+        for row in (inner, H + inner)
+    )
+    return real, -imag if conj else imag
+
+
 def iota(dim):
     return lax.broadcasted_iota(jnp.int32, (STEP, W), dim)
 
@@ -85,8 +150,16 @@
     return jnp.where(iota(1) >= col, full[part, rows, :W], full[part, rows, W:])
 
 
+def at_core():
+    return lax.axis_index("cuts")
+
+
+def spread(offsets, which):
+    return jnp.broadcast_to(offsets[0:1, which : which + 1], (STEP, W))
+
+
 def encode_kernel(offsets, live, own, coded):
-    col = offsets[0, 1]
+    col = spread(offsets, 1)
     held = own.at[:, 0]
     peak = jnp.zeros((8, W), jnp.float32)
     for start in range(0, W, STEP):
@@ -109,17 +182,17 @@
     coded[1, pl.ds(W, HEAD), :] = jnp.full((HEAD, W), flag, jnp.int32).astype(jnp.int16)
 
 
-def mixed_kernel(before, core, live, own, measured, coded, mixed):
+def mixed_kernel(before, live, own, measured, coded, mixed):
     encode_kernel(before, live, own, coded)
 
-    @pl.when(core[0] == 0)
+    @pl.when(at_core() == 0)
     def _():
         for start in range(0, W, STEP):
             rows = pl.ds(start, STEP)
             scaled = jnp.round(measured[0, rows, :] * (1.0 / MEASURED_STEP))
             mixed[0, rows, :] = scaled.astype(jnp.int32).astype(jnp.int16)
 
-    @pl.when(core[0] != 0)
+    @pl.when(at_core() != 0)
     def _():
         mixed[...] = coded[...]
 
@@ -136,20 +209,27 @@
     return coded[part, rows, :].astype(jnp.int32).astype(jnp.float32) * gain
 
 
-def roll_kernel(offsets, before, core, illumination, rolled):
-    row = lax.rem(jnp.where(core[0] == 0, before[0, 0], offsets[0, 0]), W)
-    col = lax.rem(jnp.where(core[0] == 0, before[0, 1], offsets[0, 1]), W)
+def roll_kernel(offsets, before, illumination, rolled):
+    row = lax.rem(jnp.where(at_core() == 0, before[0, 0], offsets[0, 0]), W)
+    col = lax.rem(jnp.where(at_core() == 0, before[0, 1], offsets[0, 1]), W)
     for part in range(2):
         rolled[part] = pltpu.roll(pltpu.roll(illumination[part], row, 0), col, 1)
 
 
+def multiplied(wave, patch):
+    def rows_of(rows, start):
+        wave_real, wave_imag = wave[0, rows, :].astype(jnp.float32), wave[1, rows, :].astype(jnp.float32)
+        patch_real, patch_imag = patch(0, rows, start), patch(1, rows, start)
+        return wave_real * patch_real - wave_imag * patch_imag, wave_real * patch_imag + wave_imag * patch_real
+
+    return rows_of
+
+
 def times_patch(wave, patch, out):
+    product_of = multiplied(wave, patch)
     for start in range(0, W, STEP):
         rows = pl.ds(start, STEP)
-        wave_real, wave_imag = wave[0, rows, :].astype(jnp.float32), wave[1, rows, :].astype(jnp.float32)
-        patch_real, patch_imag = patch(0, rows, start), patch(1, rows, start)
-        out[0, rows, :] = wave_real * patch_real - wave_imag * patch_imag
-        out[1, rows, :] = wave_real * patch_imag + wave_imag * patch_real
+        out[0, rows, :], out[1, rows, :] = product_of(rows, start)
 
 
 def chosen(row, upper, lower):
@@ -158,24 +238,27 @@
     )
 
 
-def first_slice(rolled, patch, prop, psi, chi):
-    times_patch(rolled, patch, chi)
-    out_real, out_imag = transform(chi[0], chi[1], prop, False)
-    psi[0] = out_real.astype(jnp.bfloat16)
-    psi[1] = out_imag.astype(jnp.bfloat16)
-
-
-def first_kernel(offsets, before, core, direct, own, rolled, prop, psi, chi):
-    @pl.when(core[0] == 0)
+def first_slice(rolled, patch, prop, psi, ops, acc):
+    propagate(multiplied(rolled, patch), prop, ops, acc, 3, False)
+    for start in range(0, W, STEP):
+        rows = pl.ds(start, STEP)
+        real, imag = propagated(acc, start, False)
+        psi[0, rows, :] = real.astype(jnp.bfloat16)
+        psi[1, rows, :] = imag.astype(jnp.bfloat16)
+
+
+def first_kernel(offsets, before, direct, own, rolled, prop, psi, ops, acc):
+    @pl.when(at_core() == 0)
     def _():
         gain = gain_of(direct)
         local = own.at[:, 0]
+        col = spread(before, 1)
         patch = chosen(
-            before[0, 0],
-            lambda part, rows: windowed(local, part, rows, before[0, 1]),
+            spread(before, 0),
+            lambda part, rows: windowed(local, part, rows, col),
             lambda part, rows: decoded(direct, part, rows, gain),
         )
-        first_slice(rolled, patch, prop, psi, chi)
+        first_slice(rolled, patch, prop, psi, ops, acc)
 
 
 def keeping(given, patch):
@@ -194,8 +277,8 @@
     field[1] = out_imag
 
 
-def second_kernel(offsets, before, core, crossed, edge, rolled, early, prop, far, psi, patch, field, chi):
-    row = jnp.where(core[0] == 0, before[0, 0], offsets[0, 0])
+def second_kernel(offsets, before, crossed, edge, rolled, early, prop, far, psi, patch, field, chi, ops, acc):
+    row = jnp.where(at_core() == 0, spread(before, 0), spread(offsets, 0))
     gain_crossed, gain_edge = gain_of(crossed), gain_of(edge)
     given = chosen(
         row,
@@ -203,27 +286,14 @@
         lambda part, rows: decoded(crossed, part, rows, gain_crossed),
     )
 
-    @pl.when(core[0] == 0)
+    @pl.when(at_core() == 0)
     def _():
         psi[...] = early[...]
         second_slice(given, psi, far, patch, field, chi)
 
-    @pl.when(core[0] != 0)
-    def _():
-        first_slice(rolled, given, prop, psi, chi)
-
-
-def late_kernel(offsets, core, border, own, psi, far, patch, field, chi):
-    @pl.when(core[0] != 0)
-    def _():
-        gain_border = gain_of(border)
-        local = own.at[:, 0]
-        last = chosen(
-            offsets[0, 0],
-            lambda part, rows: decoded(border, part, rows, gain_border),
-            lambda part, rows: windowed(local, part, rows, offsets[0, 1]),
-        )
-        second_slice(last, psi, far, patch, field, chi)
+    @pl.when(at_core() != 0)
+    def _():
+        first_slice(rolled, given, prop, psi, ops, acc)
 
 
 def conj_times(first, real, imag, out):
@@ -236,8 +306,21 @@
 
 
 def third_kernel(
-    core, live, direct, border, measured, field, late_field, psi, patch, late_patch, rolled, prop, far, send, stay, chi, half
+    offsets, live, direct, border, own, measured, field, psi, patch, rolled, prop, far, send, stay,
+    chi, half, late_patch, late_field, ops, acc,
 ):
+    @pl.when(at_core() != 0)
+    def _():
+        gain_border = gain_of(border)
+        local = own.at[:, 0]
+        col = spread(offsets, 1)
+        last = chosen(
+            spread(offsets, 0),
+            lambda part, rows: decoded(border, part, rows, gain_border),
+            lambda part, rows: windowed(local, part, rows, col),
+        )
+        second_slice(last, psi, far, late_patch, late_field, chi)
+
     def residue(field, target, alive):
         for start in range(0, W, STEP):
             rows = pl.ds(start, STEP)
@@ -246,41 +329,56 @@
             chi[0, rows, :] = weight * real
             chi[1, rows, :] = weight * imag
 
-    @pl.when(core[0] == 0)
+    @pl.when(at_core() == 0)
     def _():
         head = head_of(direct, 1)
         residue(field, lambda rows: border[0, rows, :].astype(jnp.int32).astype(jnp.float32) * MEASURED_STEP, head)
 
-    @pl.when(core[0] != 0)
+    @pl.when(at_core() != 0)
     def _():
         residue(late_field, lambda rows: measured[0, rows, :], jnp.where(live[0] > 0, 1.0, 0.0))
 
     real, imag = transform(chi[0], chi[1], far, True)
 
-    @pl.when(core[0] == 0)
+    @pl.when(at_core() == 0)
     def _():
         conj_times(patch, real, imag, half)
         conj_times(psi, real, imag, send)
 
-    @pl.when(core[0] != 0)
+    @pl.when(at_core() != 0)
     def _():
         conj_times(late_patch, real, imag, half)
         conj_times(psi, real, imag, stay)
 
-    real, imag = transform(half[0].astype(jnp.float32), half[1].astype(jnp.float32), prop, True)
-
-    @pl.when(core[0] == 0)
-    def _():
-        conj_times(rolled, real, imag, stay)
-
-    @pl.when(core[0] != 0)
-    def _():
-        conj_times(rolled, real, imag, send)
-
-
-def place_kernel(offsets, before, core, stay, came, out, staged, sems):
-    row, col = offsets[0, 0], offsets[0, 1]
-    row_before, col_before = before[0, 0], before[0, 1]
+    propagate(
+        lambda rows, start: (half[0, rows, :].astype(jnp.float32), half[1, rows, :].astype(jnp.float32)),
+        prop,
+        ops,
+        acc,
+        LAST_PASSES,
+        True,
+    )
+
+    def last(out):
+        for start in range(0, W, STEP):
+            rows = pl.ds(start, STEP)
+            real, imag = propagated(acc, start, True)
+            wave_real, wave_imag = rolled[0, rows, :], rolled[1, rows, :]
+            out[0, rows, :] = (wave_real * real + wave_imag * imag).astype(out.dtype)
+            out[1, rows, :] = (wave_real * imag - wave_imag * real).astype(out.dtype)
+
+    @pl.when(at_core() == 0)
+    def _():
+        last(stay)
+
+    @pl.when(at_core() != 0)
+    def _():
+        last(send)
+
+
+def place_kernel(offsets, before, stay, came, out, staged, sems):
+    row, col = spread(offsets, 0), spread(offsets, 1)
+    row_before, col_before = spread(before, 0), spread(before, 1)
 
     def place(own, spill):
         copies = []
@@ -299,11 +397,11 @@
         for copy in copies:
             copy.wait()
 
-    @pl.when(core[0] == 0)
+    @pl.when(at_core() == 0)
     def _():
         place(came, stay)
 
-    @pl.when(core[0] != 0)
+    @pl.when(at_core() != 0)
     def _():
         place(stay, came)
 
@@ -327,12 +425,12 @@
 HALF_WAVE = shaped((2, W, W), jnp.bfloat16)
 CODED = shaped((2, W + HEAD, W), jnp.int16)
 CHI = pltpu.VMEM((2, W, W), jnp.float32)
+PROPAGATE = [pltpu.VMEM((4, W, W), jnp.bfloat16), pltpu.VMEM((2, W, W), jnp.float32)]
 
 
 def on_device(transmission, illumination, measured, offsets, live_count):
     prop, far = (jnp.asarray(t) for t in tables())
     count = lax.axis_size("tile")
-    core = lax.axis_index("cuts").astype(jnp.int32)[None]
 
     def permute(value, target):
         pairs = []
@@ -343,30 +441,32 @@
         return lax.ppermute(value, ("cuts", "tile"), pairs)
 
     before = permute(offsets, lambda c, k: (c, k + 1))
-    place = (offsets, before, core)
-    encode = call(encode_kernel, CODED, "ssv")
+    place = (offsets, before)
+    encode = call(encode_kernel, CODED, "vsv")
     ahead = encode(offsets, live_count, transmission)
     direct = permute(ahead, lambda c, k: (0, k + 1) if c == 0 else (1, k - ASIDE))
-    behind, mixed = call(mixed_kernel, (CODED, CODED), "sssvv")(before, core, live_count, transmission, measured)
+    behind, mixed = call(mixed_kernel, (CODED, CODED), "vsvv")(
+        before, live_count, transmission, measured
+    )
     crossed = permute(ahead, lambda c, k: (1, k) if c == 0 else (0, k + 1))
     border = permute(mixed, lambda c, k: (0, k + 1) if c == 0 else (1, k - 1))
     edge = permute(behind, lambda c, k: (1, k - 1) if c == 0 else (0, k))
-    rolled = call(roll_kernel, WAVE, "sssv")(*place, illumination)
-    early = call(first_kernel, HALF_WAVE, "sssvvvv", [CHI])(*place, direct, transmission, rolled, prop)
-    psi, patch, field = call(second_kernel, (HALF_WAVE, WAVE, WAVE), "sss" + "v" * 6, [CHI])(
+    rolled = call(roll_kernel, WAVE, "ssv")(*place, illumination)
+    early = call(first_kernel, HALF_WAVE, "vvvvvv", PROPAGATE)(*place, direct, transmission, rolled, prop)
+    psi, patch, field = call(second_kernel, (HALF_WAVE, WAVE, WAVE), "v" * 8, [CHI, *PROPAGATE])(
         *place, crossed, edge, rolled, early, prop, far
     )
-    late_patch, late_field = call(late_kernel, (WAVE, WAVE), "ssvvvv", [CHI])(
-        offsets, core, border, transmission, psi, far
-    )
     send, stay = call(
-        third_kernel, (HALF_WAVE, HALF_WAVE), "ss" + "v" * 11, [CHI, pltpu.VMEM((2, W, W), jnp.bfloat16)]
-    )(core, live_count, direct, border, measured, field, late_field, psi, patch, late_patch, rolled, prop, far)
+        third_kernel,
+        (HALF_WAVE, HALF_WAVE),
+        "vs" + "v" * 10,
+        [CHI, pltpu.VMEM((2, W, W), jnp.bfloat16), CHI, CHI, *PROPAGATE],
+    )(offsets, live_count, direct, border, transmission, measured, field, psi, patch, rolled, prop, far)
     came = permute(send, lambda c, k: (1 - c, k))
     return call(
         place_kernel,
         shaped(transmission.shape, jnp.float32),
-        "sssvv",
+        "vvvv",
         [pltpu.VMEM(transmission.shape, jnp.float32), pltpu.SemaphoreType.DMA((W // FLUSH,))],
         ANY,
     )(*place, stay, came)

time: 36.3 us -> 33.7 us (0.928)
  Pallas kernels: 10.8 us -> 6.92 us
  waiting for transfers between devices: 3.92 us -> 5.45 us
  starting transfers between devices: 19.5 us -> 19.1 us
    pallas_call x7 -> x6, Pallas kernels: 10 us -> 6.66 us  [the longest x1 3.34 us: on_device(): call(third_kernel, (HALF_WAVE, HALF_WAVE), 'vs' + 'v' * 10, [CHI, pltpu.V...]
    ppermute x6, waiting for transfers between devices: 3.92 us -> 5.45 us  [permute(): return lax.ppermute(value, ('cuts', 'tile'), pairs)]
    pallas_call x1, Pallas kernels: 0.74 us -> 0.26 us  [on_device(): ahead = encode(offsets, live_count, transmission)]
  transfers between devices with their start and end apart: 6 -> 6, of which waited for: 3 -> 4; matrix products, arithmetic and copies ran while one was open for 0% -> 0% of each run, Pallas kernels for 13% -> 7%
where the time goes in v3:
time: 33.7 us; the launch traced here: 33.5 us
  starting transfers between devices  19.1 us (57%)
  Pallas kernels  6.92 us (21%)
  waiting for transfers between devices  5.45 us (16%)
  local copies, waits for them, and re-layouts  1.25 us (4%)
  between operations  0.76 us (2%)
    ppermute x6, starting transfers between devices, permute(): return lax.ppermute(value, ('cuts', 'tile'), pairs)  19.1 us
    ppermute x6, waiting for transfers between devices, permute(): return lax.ppermute(value, ('cuts', 'tile'), pairs)  5.45 us
    pallas_call x1, Pallas kernels, on_device(): call(third_kernel, (HALF_WAVE, HALF_WAVE), 'vs' + 'v' * 10, [CHI, pltpu.V...  3.34 us
    unnamed x14, local copies, waits for them, and re-layouts  1.25 us
    pallas_call x1, Pallas kernels, on_device(): call(second_kernel, (HALF_WAVE, WAVE, WAVE), 'v' * 8, [CHI, *PROPAGATE])  1.13 us
    pallas_call x1, Pallas kernels, on_device(): call(place_kernel, shaped(transmission.shape, jnp.float32), 'vvvv', [pltp...  1.11 us
    pallas_call x1, Pallas kernels, on_device(): rolled = call(roll_kernel, WAVE, 'ssv')(*place, illumination)  0.78 us
  transfers between devices with their start and end apart: 6, of which 4 were waited for; matrix products, arithmetic and copies ran while one was open for 0% of the time, Pallas kernels for 7%

profile of v3, /device:TPU:1, one launch (start us, length us, event | category | flops | bytes accessed | tf_op | source)
XLA Modules:
  0.0 33.5 jit_solution(10498630315621350453)
XLA Ops:
  0.0 0.0 copy-start.6
  0.0 2.0 %collective-permute-start = (s32[1,2]{1,0:T(1,128)}, s32[1,2]{1,0:T(1,128)S(1)}, u32[]{:S(2)}, u32[]{:S(2)}) collective-permute-start(s32[1,2]{1,0:T(1,128)} %offsets.11), channel_id=1, source_target_pairs={{0,1},{1,2},{2,3},{3,4},{4,5},{5,6},{6,7},{7,8},{8,9},{9,10},{10,1... | collective-permute-start | bytes 32 | tf_op jit(solution)/shard_map/ppermute | solution.py:441
  2.7 0.0 copy-done.6
  2.7 0.0 copy-start
  2.7 1.2 %copy-done = f32[2,1,256,512]{3,2,1,0:T(8,128)S(1)} copy-done((f32[2,1,256,512]{3,2,1,0:T(8,128)S(1)}, f32[2,1,256,512]{3,2,1,0:T(8,128)}, u32[]{:S(2)}) %copy-start) | copy-done | bytes 1048600
  3.9 0.0 copy-start.1
  3.9 0.0 copy-start.4
  3.9 0.0 copy-start.5
  3.9 0.3 shard_map.73
  4.2 0.0 copy-start.2
  4.2 2.1 %collective-permute-start.3 = (s16[2,272,256]{2,1,0:T(8,128)(2,1)S(1)}, s16[2,272,256]{2,1,0:T(8,128)(2,1)S(1)}, u32[]{:S(2)}, u32[]{:S(2)}) collective-permute-start(s16[2,272,256]{2,1,0:T(8,128)(2,1)S(1)} %shard_map.73), channel_id=1, source_target_pairs={{0,128},{1,129},{2,130},{3,131},{4,132},{5,133},{6,134},{7,135},{8... | collective-permute-start | bytes 835592 | tf_op jit(solution)/shard_map/ppermute | solution.py:441
  6.3 5.6 %collective-permute-start.1 = (s16[2,272,256]{2,1,0:T(8,128)(2,1)S(1)}, s16[2,272,256]{2,1,0:T(8,128)(2,1)S(1)}, u32[]{:S(2)}, u32[]{:S(2)}) collective-permute-start(s16[2,272,256]{2,1,0:T(8,128)(2,1)S(1)} %shard_map.73), channel_id=1, source_target_pairs={{0,1},{1,2},{2,3},{3,4},{4,5},{5,6},{6,7},{7,8},{8,9},{9,10},{10,1... | collective-permute-start | bytes 835592 | tf_op jit(solution)/shard_map/ppermute | solution.py:441
  11.9 0.3 collective-permute-done.before
  12.2 0.0 copy-done.1
  12.2 0.0 copy-done.4
  12.2 0.3 shard_map.74
  12.5 1.6 %collective-permute-start.4 = (s16[2,272,256]{2,1,0:T(8,128)(2,1)S(1)}, s16[2,272,256]{2,1,0:T(8,128)(2,1)S(1)}, u32[]{:S(2)}, u32[]{:S(2)}) collective-permute-start(s16[2,272,256]{2,1,0:T(8,128)(2,1)S(1)} %get-tuple-element.13), channel_id=1, source_target_pairs={{0,255},{1,128},{2,129},{3,130},{4,131},{5,132},{6,133},{7,134},{8... | collective-permute-start | bytes 835592 | tf_op jit(solution)/shard_map/ppermute | solution.py:441
  14.1 2.7 %collective-permute-start.2 = (s16[2,272,256]{2,1,0:T(8,128)(2,1)S(1)}, s16[2,272,256]{2,1,0:T(8,128)(2,1)S(1)}, u32[]{:S(2)}, u32[]{:S(2)}) collective-permute-start(s16[2,272,256]{2,1,0:T(8,128)(2,1)S(1)} %get-tuple-element.12), channel_id=1, source_target_pairs={{0,1},{1,2},{2,3},{3,4},{4,5},{5,6},{6,7},{7,8},{8,9},{9,10},{10,1... | collective-permute-start | bytes 835592 | tf_op jit(solution)/shard_map/ppermute | solution.py:441
  16.9 0.0 copy-done.5
  16.9 0.8 %shard_map.75.rolled = f32[2,256,256]{2,1,0:T(8,128)S(1)} custom-call(s32[1,2]{1,0:T(1,128)S(1)} %copy-done.6, s32[1,2]{1,0:T(1,128)S(1)} %collective-permute-done.before, f32[2,256,256]{2,1,0:T(8,128)S(1)} %copy-done.5), custom_call_target="tpu_custom_call" | custom-call | tf_op jit(solution)/shard_map/pallas_call | solution.py:454
  17.6 0.0 copy-start.3
  17.7 0.0 collective-permute-done.1.direct
  17.7 0.0 copy-done.2
  17.7 0.0 collective-permute-done.3.crossed
  17.7 2.8 %collective-permute-done.4.edge = s16[2,272,256]{2,1,0:T(8,128)(2,1)S(1)} collective-permute-done((s16[2,272,256]{2,1,0:T(8,128)(2,1)S(1)}, s16[2,272,256]{2,1,0:T(8,128)(2,1)S(1)}, u32[]{:S(2)}, u32[]{:S(2)}) %collective-permute-start.4) | collective-permute-done | bytes 278560 | tf_op jit(solution)/shard_map/ppermute | solution.py:441
  20.6 0.0 copy-done.3
  20.6 1.1 %shard_map.77 = (bf16[2,256,256]{2,1,0:T(8,128)(2,1)S(1)}, f32[2,256,256]{2,1,0:T(8,128)S(1)}, f32[2,256,256]{2,1,0:T(8,128)S(1)}) custom-call(s32[1,2]{1,0:T(1,128)S(1)} %copy-done.6, s32[1,2]{1,0:T(1,128)S(1)} %collective-permute-done.before, s16[2,272,256]{2,1,0:T(8,128)(2,1)S(1)} %collective-permute-done.3.crossed, ...), custom_call_target="tpu_custom_call" | custom-call | tf_op jit(solution)/shard_map/pallas_call | solution.py:456
  21.7 1.2 %collective-permute-done.2.border = s16[2,272,256]{2,1,0:T(8,128)(2,1)S(1)} collective-permute-done((s16[2,272,256]{2,1,0:T(8,128)(2,1)S(1)}, s16[2,272,256]{2,1,0:T(8,128)(2,1)S(1)}, u32[]{:S(2)}, u32[]{:S(2)}) %collective-permute-start.2) | collective-permute-done | bytes 278560 | tf_op jit(solution)/shard_map/ppermute | solution.py:441
  22.8 3.3 %shard_map.78 = (bf16[2,256,256]{2,1,0:T(8,128)(2,1)S(1)}, bf16[2,256,256]{2,1,0:T(8,128)(2,1)S(1)}) custom-call(s32[1,2]{1,0:T(1,128)S(1)} %copy-done.6, s32[1]{0:T(128)S(6)} %copy.8.live, s16[2,272,256]{2,1,0:T(8,128)(2,1)S(1)} %collective-permute-done.1.direct, s16[2,272,256]{2,1,0:T(8,128)(2,1)S(1)} %collective-permute-done.2.border, ...), custom_call_target="tpu_custom_call" | custom-call | tf_op jit(solution)/shard_map/pallas_call | solution.py:459
  26.2 5.1 %collective-permute-start.5 = (bf16[2,256,256]{2,1,0:T(8,128)(2,1)S(1)}, bf16[2,256,256]{2,1,0:T(8,128)(2,1)S(1)}, u32[]{:S(2)}, u32[]{:S(2)}) collective-permute-start(bf16[2,256,256]{2,1,0:T(8,128)(2,1)S(1)} %get-tuple-element.18), channel_id=1, source_target_pairs={{0,128},{1,129},{2,130},{3,131},{4,132},{5,133},{6,134},{7,135},{8... | collective-permute-start | bytes 786440 | tf_op jit(solution)/shard_map/ppermute | solution.py:441
  31.3 1.2 %collective-permute-done.5.came = bf16[2,256,256]{2,1,0:T(8,128)(2,1)S(1)} collective-permute-done((bf16[2,256,256]{2,1,0:T(8,128)(2,1)S(1)}, bf16[2,256,256]{2,1,0:T(8,128)(2,1)S(1)}, u32[]{:S(2)}, u32[]{:S(2)}) %collective-permute-start.5) | collective-permute-done | bytes 262176 | tf_op jit(solution)/shard_map/ppermute | solution.py:441
  32.4 1.1 %shard_map.79 = f32[2,1,256,512]{3,2,1,0:T(8,128)} custom-call(s32[1,2]{1,0:T(1,128)S(1)} %copy-done.6, s32[1,2]{1,0:T(1,128)S(1)} %collective-permute-done.before, bf16[2,256,256]{2,1,0:T(8,128)(2,1)S(1)} %get-tuple-element.17.stay, bf16[2,256,256]{2,1,0:T(8,128)(2,1)S(1)} %collective-permute-done.5.came), custom_call_target="tpu_custom_call" | custom-call | tf_op jit(solution)/shard_map/pallas_call | solution.py:466
  (1 shorter events, 0.0 us)
Async XLA Ops:
  0.0 2.7 %copy-start.6 = (s32[1,2]{1,0:T(1,128)S(1)}, s32[1,2]{1,0:T(1,128)}, u32[]{:S(2)}) copy-start(s32[1,2]{1,0:T(1,128)} %offsets.11) | copy-start | bytes 28
  0.0 12.2 %collective-permute-start = (s32[1,2]{1,0:T(1,128)}, s32[1,2]{1,0:T(1,128)S(1)}, u32[]{:S(2)}, u32[]{:S(2)}) collective-permute-start(s32[1,2]{1,0:T(1,128)} %offsets.11), channel_id=1, source_target_pairs={{0,1},{1,2},{2,3},{3,4},{4,5},{5,6},{6,7},{7,8},{8,9},{9,10},{10,1... | collective-permute-start | bytes 32 | tf_op jit(solution)/shard_map/ppermute | solution.py:441
  2.7 1.2 %copy-start = (f32[2,1,256,512]{3,2,1,0:T(8,128)S(1)}, f32[2,1,256,512]{3,2,1,0:T(8,128)}, u32[]{:S(2)}) copy-start(f32[2,1,256,512]{3,2,1,0:T(8,128)} %own.7) | copy-start | bytes 3145732
  3.9 8.3 %copy-start.1 = (f32[2,1,256,512]{3,2,1,0:T(8,128)S(1)}, f32[2,1,256,512]{3,2,1,0:T(8,128)}, u32[]{:S(2)}) copy-start(f32[2,1,256,512]{3,2,1,0:T(8,128)} %own.7) | copy-start | bytes 3145732
  3.9 8.3 %copy-start.4 = (f32[1,256,256]{2,1,0:T(8,128)S(1)}, f32[1,256,256]{2,1,0:T(8,128)}, u32[]{:S(2)}) copy-start(f32[1,256,256]{2,1,0:T(8,128)} %measured.3) | copy-start | bytes 786436
  3.9 12.9 %copy-start.5 = (f32[2,256,256]{2,1,0:T(8,128)S(1)}, f32[2,256,256]{2,1,0:T(8,128)}, u32[]{:S(2)}) copy-start(f32[2,256,256]{2,1,0:T(8,128)} %illumination.1) | copy-start | bytes 1572868
  4.2 13.5 %copy-start.2 = (bf16[8,256,256]{2,1,0:T(8,128)(2,1)S(1)}, bf16[8,256,256]{2,1,0:T(8,128)(2,1)}, u32[]{:S(2)}) copy-start(bf16[8,256,256]{2,1,0:T(8,128)(2,1)} %constant.4.clone.prop) | copy-start | bytes 3145732
  4.2 13.5 %collective-permute-start.3 = (s16[2,272,256]{2,1,0:T(8,128)(2,1)S(1)}, s16[2,272,256]{2,1,0:T(8,128)(2,1)S(1)}, u32[]{:S(2)}, u32[]{:S(2)}) collective-permute-start(s16[2,272,256]{2,1,0:T(8,128)(2,1)S(1)} %shard_map.73), channel_id=1, source_target_pairs={{0,128},{1,129},{2,130},{3,131},{4,132},{5,133},{6,134},{7,135},{8... | collective-permute-start | bytes 835592 | tf_op jit(solution)/shard_map/ppermute | solution.py:441
  6.3 11.3 %collective-permute-start.1 = (s16[2,272,256]{2,1,0:T(8,128)(2,1)S(1)}, s16[2,272,256]{2,1,0:T(8,128)(2,1)S(1)}, u32[]{:S(2)}, u32[]{:S(2)}) collective-permute-start(s16[2,272,256]{2,1,0:T(8,128)(2,1)S(1)} %shard_map.73), channel_id=1, source_target_pairs={{0,1},{1,2},{2,3},{3,4},{4,5},{5,6},{6,7},{7,8},{8,9},{9,10},{10,1... | collective-permute-start | bytes 835592 | tf_op jit(solution)/shard_map/ppermute | solution.py:441
  12.5 8.1 %collective-permute-start.4 = (s16[2,272,256]{2,1,0:T(8,128)(2,1)S(1)}, s16[2,272,256]{2,1,0:T(8,128)(2,1)S(1)}, u32[]{:S(2)}, u32[]{:S(2)}) collective-permute-start(s16[2,272,256]{2,1,0:T(8,128)(2,1)S(1)} %get-tuple-element.13), channel_id=1, source_target_pairs={{0,255},{1,128},{2,129},{3,130},{4,131},{5,132},{6,133},{7,134},{8... | collective-permute-start | bytes 835592 | tf_op jit(solution)/shard_map/ppermute | solution.py:441
  14.1 8.7 %collective-permute-start.2 = (s16[2,272,256]{2,1,0:T(8,128)(2,1)S(1)}, s16[2,272,256]{2,1,0:T(8,128)(2,1)S(1)}, u32[]{:S(2)}, u32[]{:S(2)}) collective-permute-start(s16[2,272,256]{2,1,0:T(8,128)(2,1)S(1)} %get-tuple-element.12), channel_id=1, source_target_pairs={{0,1},{1,2},{2,3},{3,4},{4,5},{5,6},{6,7},{7,8},{8,9},{9,10},{10,1... | collective-permute-start | bytes 835592 | tf_op jit(solution)/shard_map/ppermute | solution.py:441
  17.6 2.9 %copy-start.3 = (bf16[6,256,256]{2,1,0:T(8,128)(2,1)S(1)}, bf16[6,256,256]{2,1,0:T(8,128)(2,1)}, u32[]{:S(2)}) copy-start(bf16[6,256,256]{2,1,0:T(8,128)(2,1)} %constant.5.clone.far) | copy-start | bytes 2359300
  26.2 6.2 %collective-permute-start.5 = (bf16[2,256,256]{2,1,0:T(8,128)(2,1)S(1)}, bf16[2,256,256]{2,1,0:T(8,128)(2,1)S(1)}, u32[]{:S(2)}, u32[]{:S(2)}) collective-permute-start(bf16[2,256,256]{2,1,0:T(8,128)(2,1)S(1)} %get-tuple-element.18), channel_id=1, source_target_pairs={{0,128},{1,129},{2,130},{3,131},{4,132},{5,133},{6,134},{7,135},{8... | collective-permute-start | bytes 786440 | tf_op jit(solution)/shard_map/ppermute | solution.py:441

commit v4 on v3

--- a/solution.py
+++ b/solution.py
@@ -305,9 +305,26 @@
         out[1, rows, :] = (first_real * imag[keep] - first_imag * real[keep]).astype(out.dtype)
 
 
+def last_slice(half, rolled, prop, out, ops, acc):
+    propagate(
+        lambda rows, start: (half[0, rows, :].astype(jnp.float32), half[1, rows, :].astype(jnp.float32)),
+        prop,
+        ops,
+        acc,
+        LAST_PASSES,
+        True,
+    )
+    for start in range(0, W, STEP):
+        rows = pl.ds(start, STEP)
+        real, imag = propagated(acc, start, True)
+        wave_real, wave_imag = rolled[0, rows, :], rolled[1, rows, :]
+        out[0, rows, :] = (wave_real * real + wave_imag * imag).astype(out.dtype)
+        out[1, rows, :] = (wave_real * imag - wave_imag * real).astype(out.dtype)
+
+
 def third_kernel(
-    offsets, live, direct, border, own, measured, field, psi, patch, rolled, prop, far, send, stay,
-    chi, half, late_patch, late_field, ops, acc,
+    offsets, live, direct, border, own, measured, field, psi, patch, rolled, prop, far, send, early, half,
+    chi, late_patch, late_field, ops, acc,
 ):
     @pl.when(at_core() != 0)
     def _():
@@ -348,32 +365,18 @@
     @pl.when(at_core() != 0)
     def _():
         conj_times(late_patch, real, imag, half)
-        conj_times(psi, real, imag, stay)
-
-    propagate(
-        lambda rows, start: (half[0, rows, :].astype(jnp.float32), half[1, rows, :].astype(jnp.float32)),
-        prop,
-        ops,
-        acc,
-        LAST_PASSES,
-        True,
-    )
-
-    def last(out):
-        for start in range(0, W, STEP):
-            rows = pl.ds(start, STEP)
-            real, imag = propagated(acc, start, True)
-            wave_real, wave_imag = rolled[0, rows, :], rolled[1, rows, :]
-            out[0, rows, :] = (wave_real * real + wave_imag * imag).astype(out.dtype)
-            out[1, rows, :] = (wave_real * imag - wave_imag * real).astype(out.dtype)
-
-    @pl.when(at_core() == 0)
-    def _():
-        last(stay)
-
-    @pl.when(at_core() != 0)
-    def _():
-        last(send)
+        conj_times(psi, real, imag, early)
+        last_slice(half, rolled, prop, send, ops, acc)
+
+
+def fourth_kernel(half, rolled, early, prop, stay, ops, acc):
+    @pl.when(at_core() == 0)
+    def _():
+        last_slice(half, rolled, prop, stay, ops, acc)
+
+    @pl.when(at_core() != 0)
+    def _():
+        stay[...] = early[...]
 
 
 def place_kernel(offsets, before, stay, came, out, staged, sems):
@@ -456,13 +459,11 @@
     psi, patch, field = call(second_kernel, (HALF_WAVE, WAVE, WAVE), "v" * 8, [CHI, *PROPAGATE])(
         *place, crossed, edge, rolled, early, prop, far
     )
-    send, stay = call(
-        third_kernel,
-        (HALF_WAVE, HALF_WAVE),
-        "vs" + "v" * 10,
-        [CHI, pltpu.VMEM((2, W, W), jnp.bfloat16), CHI, CHI, *PROPAGATE],
+    send, early_stay, half = call(
+        third_kernel, (HALF_WAVE, HALF_WAVE, HALF_WAVE), "vs" + "v" * 10, [CHI, CHI, CHI, *PROPAGATE]
     )(offsets, live_count, direct, border, transmission, measured, field, psi, patch, rolled, prop, far)
     came = permute(send, lambda c, k: (1 - c, k))
+    stay = call(fourth_kernel, HALF_WAVE, "vvvv", PROPAGATE)(half, rolled, early_stay, prop)
     return call(
         place_kernel,
         shaped(transmission.shape, jnp.float32),

time: 33.7 us -> 33.1 us (0.982)
  starting transfers between devices: 19.1 us -> 18.7 us
    ppermute x6, starting transfers between devices: 19.1 us -> 18.7 us  [permute(): return lax.ppermute(value, ('cuts', 'tile'), pairs)]
    pallas_call x1 -> x2, Pallas kernels: 3.34 us -> 3.25 us  [the longest x1 3.23 us: on_device(): call(third_kernel, (HALF_WAVE, HALF_WAVE, HALF_WAVE), 'vs' + 'v' * 10, [C...]
  transfers between devices with their start and end apart: 6 -> 6, of which waited for: 4 -> 4; matrix products, arithmetic and copies ran while one was open for 0% -> 0% of each run, Pallas kernels for 7% -> 8%
where the time goes in v4:
time: 33.1 us; the launch traced here: 32.9 us
  starting transfers between devices  18.7 us (56%)
  Pallas kernels  6.83 us (21%)
  waiting for transfers between devices  5.43 us (16%)
  local copies, waits for them, and re-layouts  1.25 us (4%)
  between operations  0.77 us (2%)
    ppermute x6, starting transfers between devices, permute(): return lax.ppermute(value, ('cuts', 'tile'), pairs)  18.7 us
    ppermute x6, waiting for transfers between devices, permute(): return lax.ppermute(value, ('cuts', 'tile'), pairs)  5.43 us
    pallas_call x1, Pallas kernels, on_device(): call(third_kernel, (HALF_WAVE, HALF_WAVE, HALF_WAVE), 'vs' + 'v' * 10, [C...  3.23 us
    unnamed x14, local copies, waits for them, and re-layouts  1.25 us
    pallas_call x1, Pallas kernels, on_device(): call(second_kernel, (HALF_WAVE, WAVE, WAVE), 'v' * 8, [CHI, *PROPAGATE])  1.13 us
    pallas_call x1, Pallas kernels, on_device(): call(place_kernel, shaped(transmission.shape, jnp.float32), 'vvvv', [pltp...  1.11 us
    pallas_call x1, Pallas kernels, on_device(): rolled = call(roll_kernel, WAVE, 'ssv')(*place, illumination)  0.78 us
  transfers between devices with their start and end apart: 6, of which 4 were waited for; matrix products, arithmetic and copies ran while one was open for 0% of the time, Pallas kernels for 8%

profile of v4, /device:TPU:1, one launch (start us, length us, event | category | flops | bytes accessed | tf_op | source)
XLA Modules:
  0.0 32.9 jit_solution(15223274149808255140)
XLA Ops:
  0.0 0.0 copy-start.6
  0.0 2.0 %collective-permute-start = (s32[1,2]{1,0:T(1,128)}, s32[1,2]{1,0:T(1,128)S(1)}, u32[]{:S(2)}, u32[]{:S(2)}) collective-permute-start(s32[1,2]{1,0:T(1,128)} %offsets.11), channel_id=1, source_target_pairs={{0,1},{1,2},{2,3},{3,4},{4,5},{5,6},{6,7},{7,8},{8,9},{9,10},{10,1... | collective-permute-start | bytes 32 | tf_op jit(solution)/shard_map/ppermute | solution.py:444
  2.7 0.0 copy-done.6
  2.7 0.0 copy-start
  2.7 1.2 %copy-done = f32[2,1,256,512]{3,2,1,0:T(8,128)S(1)} copy-done((f32[2,1,256,512]{3,2,1,0:T(8,128)S(1)}, f32[2,1,256,512]{3,2,1,0:T(8,128)}, u32[]{:S(2)}) %copy-start) | copy-done | bytes 1048600
  3.9 0.0 copy-start.1
  3.9 0.0 copy-start.4
  3.9 0.0 copy-start.5
  3.9 0.3 shard_map.73
  4.2 0.0 copy-start.2
  4.2 2.1 %collective-permute-start.3 = (s16[2,272,256]{2,1,0:T(8,128)(2,1)S(1)}, s16[2,272,256]{2,1,0:T(8,128)(2,1)S(1)}, u32[]{:S(2)}, u32[]{:S(2)}) collective-permute-start(s16[2,272,256]{2,1,0:T(8,128)(2,1)S(1)} %shard_map.73), channel_id=1, source_target_pairs={{0,128},{1,129},{2,130},{3,131},{4,132},{5,133},{6,134},{7,135},{8... | collective-permute-start | bytes 835592 | tf_op jit(solution)/shard_map/ppermute | solution.py:444
  6.3 5.6 %collective-permute-start.1 = (s16[2,272,256]{2,1,0:T(8,128)(2,1)S(1)}, s16[2,272,256]{2,1,0:T(8,128)(2,1)S(1)}, u32[]{:S(2)}, u32[]{:S(2)}) collective-permute-start(s16[2,272,256]{2,1,0:T(8,128)(2,1)S(1)} %shard_map.73), channel_id=1, source_target_pairs={{0,1},{1,2},{2,3},{3,4},{4,5},{5,6},{6,7},{7,8},{8,9},{9,10},{10,1... | collective-permute-start | bytes 835592 | tf_op jit(solution)/shard_map/ppermute | solution.py:444
  11.9 0.3 collective-permute-done.before
  12.2 0.0 copy-done.1
  12.2 0.0 copy-done.4
  12.2 0.3 shard_map.74
  12.5 1.6 %collective-permute-start.4 = (s16[2,272,256]{2,1,0:T(8,128)(2,1)S(1)}, s16[2,272,256]{2,1,0:T(8,128)(2,1)S(1)}, u32[]{:S(2)}, u32[]{:S(2)}) collective-permute-start(s16[2,272,256]{2,1,0:T(8,128)(2,1)S(1)} %get-tuple-element.14), channel_id=1, source_target_pairs={{0,255},{1,128},{2,129},{3,130},{4,131},{5,132},{6,133},{7,134},{8... | collective-permute-start | bytes 835592 | tf_op jit(solution)/shard_map/ppermute | solution.py:444
  14.1 2.7 %collective-permute-start.2 = (s16[2,272,256]{2,1,0:T(8,128)(2,1)S(1)}, s16[2,272,256]{2,1,0:T(8,128)(2,1)S(1)}, u32[]{:S(2)}, u32[]{:S(2)}) collective-permute-start(s16[2,272,256]{2,1,0:T(8,128)(2,1)S(1)} %get-tuple-element.13), channel_id=1, source_target_pairs={{0,1},{1,2},{2,3},{3,4},{4,5},{5,6},{6,7},{7,8},{8,9},{9,10},{10,1... | collective-permute-start | bytes 835592 | tf_op jit(solution)/shard_map/ppermute | solution.py:444
  16.9 0.0 copy-done.5
  16.9 0.8 %shard_map.75.rolled = f32[2,256,256]{2,1,0:T(8,128)S(1)} custom-call(s32[1,2]{1,0:T(1,128)S(1)} %copy-done.6, s32[1,2]{1,0:T(1,128)S(1)} %collective-permute-done.before, f32[2,256,256]{2,1,0:T(8,128)S(1)} %copy-done.5), custom_call_target="tpu_custom_call" | custom-call | tf_op jit(solution)/shard_map/pallas_call | solution.py:457
  17.6 0.0 copy-start.3
  17.7 0.0 collective-permute-done.1.direct
  17.7 0.0 copy-done.2
  17.7 0.0 collective-permute-done.3.crossed
  17.7 2.8 %collective-permute-done.4.edge = s16[2,272,256]{2,1,0:T(8,128)(2,1)S(1)} collective-permute-done((s16[2,272,256]{2,1,0:T(8,128)(2,1)S(1)}, s16[2,272,256]{2,1,0:T(8,128)(2,1)S(1)}, u32[]{:S(2)}, u32[]{:S(2)}) %collective-permute-start.4) | collective-permute-done | bytes 278560 | tf_op jit(solution)/shard_map/ppermute | solution.py:444
  20.6 0.0 copy-done.3
  20.6 1.1 %shard_map.77 = (bf16[2,256,256]{2,1,0:T(8,128)(2,1)S(1)}, f32[2,256,256]{2,1,0:T(8,128)S(1)}, f32[2,256,256]{2,1,0:T(8,128)S(1)}) custom-call(s32[1,2]{1,0:T(1,128)S(1)} %copy-done.6, s32[1,2]{1,0:T(1,128)S(1)} %collective-permute-done.before, s16[2,272,256]{2,1,0:T(8,128)(2,1)S(1)} %collective-permute-done.3.crossed, ...), custom_call_target="tpu_custom_call" | custom-call | tf_op jit(solution)/shard_map/pallas_call | solution.py:459
  21.7 1.2 %collective-permute-done.2.border = s16[2,272,256]{2,1,0:T(8,128)(2,1)S(1)} collective-permute-done((s16[2,272,256]{2,1,0:T(8,128)(2,1)S(1)}, s16[2,272,256]{2,1,0:T(8,128)(2,1)S(1)}, u32[]{:S(2)}, u32[]{:S(2)}) %collective-permute-start.2) | collective-permute-done | bytes 278560 | tf_op jit(solution)/shard_map/ppermute | solution.py:444
  22.8 3.2 %shard_map.78 = (bf16[2,256,256]{2,1,0:T(8,128)(2,1)S(1)}, bf16[2,256,256]{2,1,0:T(8,128)(2,1)S(1)}, bf16[2,256,256]{2,1,0:T(8,128)(2,1)S(1)}) custom-call(s32[1,2]{1,0:T(1,128)S(1)} %copy-done.6, s32[1]{0:T(128)S(6)} %copy.8.live, s16[2,272,256]{2,1,0:T(8,128)(2,1)S(1)} %collective-permute-done.1.direct, ...), custom_call_target="tpu_custom_call" | custom-call | tf_op jit(solution)/shard_map/pallas_call | solution.py:462
  26.1 4.6 %collective-permute-start.5 = (bf16[2,256,256]{2,1,0:T(8,128)(2,1)S(1)}, bf16[2,256,256]{2,1,0:T(8,128)(2,1)S(1)}, u32[]{:S(2)}, u32[]{:S(2)}) collective-permute-start(bf16[2,256,256]{2,1,0:T(8,128)(2,1)S(1)} %get-tuple-element.20), channel_id=1, source_target_pairs={{0,128},{1,129},{2,130},{3,131},{4,132},{5,133},{6,134},{7,135},{8... | collective-permute-start | bytes 786440 | tf_op jit(solution)/shard_map/ppermute | solution.py:444
  30.7 1.1 %collective-permute-done.5.came = bf16[2,256,256]{2,1,0:T(8,128)(2,1)S(1)} collective-permute-done((bf16[2,256,256]{2,1,0:T(8,128)(2,1)S(1)}, bf16[2,256,256]{2,1,0:T(8,128)(2,1)S(1)}, u32[]{:S(2)}, u32[]{:S(2)}) %collective-permute-start.5) | collective-permute-done | bytes 262176 | tf_op jit(solution)/shard_map/ppermute | solution.py:444
  31.8 1.1 %shard_map.80 = f32[2,1,256,512]{3,2,1,0:T(8,128)} custom-call(s32[1,2]{1,0:T(1,128)S(1)} %copy-done.6, s32[1,2]{1,0:T(1,128)S(1)} %collective-permute-done.before, bf16[2,256,256]{2,1,0:T(8,128)(2,1)S(1)} %shard_map.79.stay, bf16[2,256,256]{2,1,0:T(8,128)(2,1)S(1)} %collective-permute-done.5.came), custom_call_target="tpu_custom_call" | custom-call | tf_op jit(solution)/shard_map/pallas_call | solution.py:467
  (2 shorter events, 0.0 us)
Async XLA Ops:
  0.0 2.7 %copy-start.6 = (s32[1,2]{1,0:T(1,128)S(1)}, s32[1,2]{1,0:T(1,128)}, u32[]{:S(2)}) copy-start(s32[1,2]{1,0:T(1,128)} %offsets.11) | copy-start | bytes 28
  0.0 12.2 %collective-permute-start = (s32[1,2]{1,0:T(1,128)}, s32[1,2]{1,0:T(1,128)S(1)}, u32[]{:S(2)}, u32[]{:S(2)}) collective-permute-start(s32[1,2]{1,0:T(1,128)} %offsets.11), channel_id=1, source_target_pairs={{0,1},{1,2},{2,3},{3,4},{4,5},{5,6},{6,7},{7,8},{8,9},{9,10},{10,1... | collective-permute-start | bytes 32 | tf_op jit(solution)/shard_map/ppermute | solution.py:444
  2.7 1.2 %copy-start = (f32[2,1,256,512]{3,2,1,0:T(8,128)S(1)}, f32[2,1,256,512]{3,2,1,0:T(8,128)}, u32[]{:S(2)}) copy-start(f32[2,1,256,512]{3,2,1,0:T(8,128)} %own.7) | copy-start | bytes 3145732
  3.9 8.3 %copy-start.1 = (f32[2,1,256,512]{3,2,1,0:T(8,128)S(1)}, f32[2,1,256,512]{3,2,1,0:T(8,128)}, u32[]{:S(2)}) copy-start(f32[2,1,256,512]{3,2,1,0:T(8,128)} %own.7) | copy-start | bytes 3145732
  3.9 8.3 %copy-start.4 = (f32[1,256,256]{2,1,0:T(8,128)S(1)}, f32[1,256,256]{2,1,0:T(8,128)}, u32[]{:S(2)}) copy-start(f32[1,256,256]{2,1,0:T(8,128)} %measured.3) | copy-start | bytes 786436
  3.9 12.9 %copy-start.5 = (f32[2,256,256]{2,1,0:T(8,128)S(1)}, f32[2,256,256]{2,1,0:T(8,128)}, u32[]{:S(2)}) copy-start(f32[2,256,256]{2,1,0:T(8,128)} %illumination.1) | copy-start | bytes 1572868
  4.2 13.5 %copy-start.2 = (bf16[8,256,256]{2,1,0:T(8,128)(2,1)S(1)}, bf16[8,256,256]{2,1,0:T(8,128)(2,1)}, u32[]{:S(2)}) copy-start(bf16[8,256,256]{2,1,0:T(8,128)(2,1)} %constant.4.clone.prop) | copy-start | bytes 3145732
  4.2 13.5 %collective-permute-start.3 = (s16[2,272,256]{2,1,0:T(8,128)(2,1)S(1)}, s16[2,272,256]{2,1,0:T(8,128)(2,1)S(1)}, u32[]{:S(2)}, u32[]{:S(2)}) collective-permute-start(s16[2,272,256]{2,1,0:T(8,128)(2,1)S(1)} %shard_map.73), channel_id=1, source_target_pairs={{0,128},{1,129},{2,130},{3,131},{4,132},{5,133},{6,134},{7,135},{8... | collective-permute-start | bytes 835592 | tf_op jit(solution)/shard_map/ppermute | solution.py:444
  6.3 11.3 %collective-permute-start.1 = (s16[2,272,256]{2,1,0:T(8,128)(2,1)S(1)}, s16[2,272,256]{2,1,0:T(8,128)(2,1)S(1)}, u32[]{:S(2)}, u32[]{:S(2)}) collective-permute-start(s16[2,272,256]{2,1,0:T(8,128)(2,1)S(1)} %shard_map.73), channel_id=1, source_target_pairs={{0,1},{1,2},{2,3},{3,4},{4,5},{5,6},{6,7},{7,8},{8,9},{9,10},{10,1... | collective-permute-start | bytes 835592 | tf_op jit(solution)/shard_map/ppermute | solution.py:444
  12.5 8.1 %collective-permute-start.4 = (s16[2,272,256]{2,1,0:T(8,128)(2,1)S(1)}, s16[2,272,256]{2,1,0:T(8,128)(2,1)S(1)}, u32[]{:S(2)}, u32[]{:S(2)}) collective-permute-start(s16[2,272,256]{2,1,0:T(8,128)(2,1)S(1)} %get-tuple-element.14), channel_id=1, source_target_pairs={{0,255},{1,128},{2,129},{3,130},{4,131},{5,132},{6,133},{7,134},{8... | collective-permute-start | bytes 835592 | tf_op jit(solution)/shard_map/ppermute | solution.py:444
  14.1 8.7 %collective-permute-start.2 = (s16[2,272,256]{2,1,0:T(8,128)(2,1)S(1)}, s16[2,272,256]{2,1,0:T(8,128)(2,1)S(1)}, u32[]{:S(2)}, u32[]{:S(2)}) collective-permute-start(s16[2,272,256]{2,1,0:T(8,128)(2,1)S(1)} %get-tuple-element.13), channel_id=1, source_target_pairs={{0,1},{1,2},{2,3},{3,4},{4,5},{5,6},{6,7},{7,8},{8,9},{9,10},{10,1... | collective-permute-start | bytes 835592 | tf_op jit(solution)/shard_map/ppermute | solution.py:444
  17.6 2.9 %copy-start.3 = (bf16[6,256,256]{2,1,0:T(8,128)(2,1)S(1)}, bf16[6,256,256]{2,1,0:T(8,128)(2,1)}, u32[]{:S(2)}) copy-start(bf16[6,256,256]{2,1,0:T(8,128)(2,1)} %constant.5.clone.far) | copy-start | bytes 2359300
  26.1 5.7 %collective-permute-start.5 = (bf16[2,256,256]{2,1,0:T(8,128)(2,1)S(1)}, bf16[2,256,256]{2,1,0:T(8,128)(2,1)S(1)}, u32[]{:S(2)}, u32[]{:S(2)}) collective-permute-start(bf16[2,256,256]{2,1,0:T(8,128)(2,1)S(1)} %get-tuple-element.20), channel_id=1, source_target_pairs={{0,128},{1,129},{2,130},{3,131},{4,132},{5,133},{6,134},{7,135},{8... | collective-permute-start | bytes 786440 | tf_op jit(solution)/shard_map/ppermute | solution.py:444

commit v5 on v4

--- a/solution.py
+++ b/solution.py
@@ -14,9 +14,9 @@
 H = W // 2
 HEAD = 16
 TOP = 32000.0
-STEP = 32
-ASIDE = 16
-FLUSH = 64
+STEP = 16
+ASIDE = 1
+FLUSH = 32
 LAST_PASSES = 1
 MEASURED_STEP = 5.0 / TOP
 VMEM = pl.BlockSpec(memory_space=pltpu.VMEM)
@@ -447,7 +447,7 @@
     place = (offsets, before)
     encode = call(encode_kernel, CODED, "vsv")
     ahead = encode(offsets, live_count, transmission)
-    direct = permute(ahead, lambda c, k: (0, k + 1) if c == 0 else (1, k - ASIDE))
+    direct = permute(ahead, lambda c, k: (0, k + 1) if c == 0 else (1, k ^ ASIDE))
     behind, mixed = call(mixed_kernel, (CODED, CODED), "vsvv")(
         before, live_count, transmission, measured
     )

time: 33.1 us -> 32 us (0.967)
  starting transfers between devices: 18.7 us -> 12.9 us
  waiting for transfers between devices: 5.43 us -> 10.1 us
    ppermute x6, starting transfers between devices: 18.7 us -> 12.9 us  [permute(): return lax.ppermute(value, ('cuts', 'tile'), pairs)]
    ppermute x6, waiting for transfers between devices: 5.43 us -> 10.1 us  [permute(): return lax.ppermute(value, ('cuts', 'tile'), pairs)]
where the time goes in v5:
time: 32 us; the launch traced here: 31.9 us
  starting transfers between devices  12.9 us (40%)
  waiting for transfers between devices  10.1 us (32%)
  Pallas kernels  6.82 us (21%)
  local copies, waits for them, and re-layouts  1.25 us (4%)
  between operations  0.77 us (2%)
    ppermute x6, starting transfers between devices, permute(): return lax.ppermute(value, ('cuts', 'tile'), pairs)  12.9 us
    ppermute x6, waiting for transfers between devices, permute(): return lax.ppermute(value, ('cuts', 'tile'), pairs)  10.1 us
    pallas_call x1, Pallas kernels, on_device(): call(third_kernel, (HALF_WAVE, HALF_WAVE, HALF_WAVE), 'vs' + 'v' * 10, [C...  3.22 us
    unnamed x14, local copies, waits for them, and re-layouts  1.25 us
    pallas_call x1, Pallas kernels, on_device(): call(second_kernel, (HALF_WAVE, WAVE, WAVE), 'v' * 8, [CHI, *PROPAGATE])  1.12 us
    pallas_call x1, Pallas kernels, on_device(): call(place_kernel, shaped(transmission.shape, jnp.float32), 'vvvv', [pltp...  1.12 us
    pallas_call x1, Pallas kernels, on_device(): rolled = call(roll_kernel, WAVE, 'ssv')(*place, illumination)  0.78 us
  transfers between devices with their start and end apart: 6, of which 4 were waited for; matrix products, arithmetic and copies ran while one was open for 0% of the time, Pallas kernels for 8%

profile of v5, /device:TPU:1, one launch (start us, length us, event | category | flops | bytes accessed | tf_op | source)
XLA Modules:
  0.0 31.9 jit_solution(3229769333210576654)
XLA Ops:
  0.0 0.0 copy-start.6
  0.0 2.0 %collective-permute-start = (s32[1,2]{1,0:T(1,128)}, s32[1,2]{1,0:T(1,128)S(1)}, u32[]{:S(2)}, u32[]{:S(2)}) collective-permute-start(s32[1,2]{1,0:T(1,128)} %offsets.11), channel_id=1, source_target_pairs={{0,1},{1,2},{2,3},{3,4},{4,5},{5,6},{6,7},{7,8},{8,9},{9,10},{10,1... | collective-permute-start | bytes 32 | tf_op jit(solution)/shard_map/ppermute | solution.py:444
  2.7 0.0 copy-done.6
  2.7 0.0 copy-start
  2.7 1.2 %copy-done = f32[2,1,256,512]{3,2,1,0:T(8,128)S(1)} copy-done((f32[2,1,256,512]{3,2,1,0:T(8,128)S(1)}, f32[2,1,256,512]{3,2,1,0:T(8,128)}, u32[]{:S(2)}) %copy-start) | copy-done | bytes 1048600
  3.9 0.0 copy-start.1
  3.9 0.0 copy-start.4
  3.9 0.0 copy-start.5
  3.9 0.3 shard_map.73
  4.2 0.0 copy-start.2
  4.2 2.1 %collective-permute-start.3 = (s16[2,272,256]{2,1,0:T(8,128)(2,1)S(1)}, s16[2,272,256]{2,1,0:T(8,128)(2,1)S(1)}, u32[]{:S(2)}, u32[]{:S(2)}) collective-permute-start(s16[2,272,256]{2,1,0:T(8,128)(2,1)S(1)} %shard_map.73), channel_id=1, source_target_pairs={{0,128},{1,129},{2,130},{3,131},{4,132},{5,133},{6,134},{7,135},{8... | collective-permute-start | bytes 835592 | tf_op jit(solution)/shard_map/ppermute | solution.py:444
  6.3 0.9 %collective-permute-start.1 = (s16[2,272,256]{2,1,0:T(8,128)(2,1)S(1)}, s16[2,272,256]{2,1,0:T(8,128)(2,1)S(1)}, u32[]{:S(2)}, u32[]{:S(2)}) collective-permute-start(s16[2,272,256]{2,1,0:T(8,128)(2,1)S(1)} %shard_map.73), channel_id=1, source_target_pairs={{0,1},{1,2},{2,3},{3,4},{4,5},{5,6},{6,7},{7,8},{8,9},{9,10},{10,1... | collective-permute-start | bytes 835592 | tf_op jit(solution)/shard_map/ppermute | solution.py:444
  7.3 4.9 %collective-permute-done.before = s32[1,2]{1,0:T(1,128)S(1)} collective-permute-done((s32[1,2]{1,0:T(1,128)}, s32[1,2]{1,0:T(1,128)S(1)}, u32[]{:S(2)}, u32[]{:S(2)}) %collective-permute-start) | collective-permute-done | bytes 40 | tf_op jit(solution)/shard_map/ppermute | solution.py:444
  12.2 0.0 copy-done.1
  12.2 0.0 copy-done.4
  12.2 0.3 shard_map.74
  12.5 1.6 %collective-permute-start.4 = (s16[2,272,256]{2,1,0:T(8,128)(2,1)S(1)}, s16[2,272,256]{2,1,0:T(8,128)(2,1)S(1)}, u32[]{:S(2)}, u32[]{:S(2)}) collective-permute-start(s16[2,272,256]{2,1,0:T(8,128)(2,1)S(1)} %get-tuple-element.14), channel_id=1, source_target_pairs={{0,255},{1,128},{2,129},{3,130},{4,131},{5,132},{6,133},{7,134},{8... | collective-permute-start | bytes 835592 | tf_op jit(solution)/shard_map/ppermute | solution.py:444
  14.1 1.7 %collective-permute-start.2 = (s16[2,272,256]{2,1,0:T(8,128)(2,1)S(1)}, s16[2,272,256]{2,1,0:T(8,128)(2,1)S(1)}, u32[]{:S(2)}, u32[]{:S(2)}) collective-permute-start(s16[2,272,256]{2,1,0:T(8,128)(2,1)S(1)} %get-tuple-element.13), channel_id=1, source_target_pairs={{0,1},{1,2},{2,3},{3,4},{4,5},{5,6},{6,7},{7,8},{8,9},{9,10},{10,1... | collective-permute-start | bytes 835592 | tf_op jit(solution)/shard_map/ppermute | solution.py:444
  15.8 0.0 copy-done.5
  15.8 0.8 %shard_map.75.rolled = f32[2,256,256]{2,1,0:T(8,128)S(1)} custom-call(s32[1,2]{1,0:T(1,128)S(1)} %copy-done.6, s32[1,2]{1,0:T(1,128)S(1)} %collective-permute-done.before, f32[2,256,256]{2,1,0:T(8,128)S(1)} %copy-done.5), custom_call_target="tpu_custom_call" | custom-call | tf_op jit(solution)/shard_map/pallas_call | solution.py:457
  16.6 0.0 copy-start.3
  16.6 0.0 collective-permute-done.1.direct
  16.6 0.0 copy-done.2
  16.7 0.0 collective-permute-done.3.crossed
  16.7 3.9 %collective-permute-done.4.edge = s16[2,272,256]{2,1,0:T(8,128)(2,1)S(1)} collective-permute-done((s16[2,272,256]{2,1,0:T(8,128)(2,1)S(1)}, s16[2,272,256]{2,1,0:T(8,128)(2,1)S(1)}, u32[]{:S(2)}, u32[]{:S(2)}) %collective-permute-start.4) | collective-permute-done | bytes 278560 | tf_op jit(solution)/shard_map/ppermute | solution.py:444
  20.6 0.0 copy-done.3
  20.6 1.1 %shard_map.77 = (bf16[2,256,256]{2,1,0:T(8,128)(2,1)S(1)}, f32[2,256,256]{2,1,0:T(8,128)S(1)}, f32[2,256,256]{2,1,0:T(8,128)S(1)}) custom-call(s32[1,2]{1,0:T(1,128)S(1)} %copy-done.6, s32[1,2]{1,0:T(1,128)S(1)} %collective-permute-done.before, s16[2,272,256]{2,1,0:T(8,128)(2,1)S(1)} %collective-permute-done.3.crossed, ...), custom_call_target="tpu_custom_call" | custom-call | tf_op jit(solution)/shard_map/pallas_call | solution.py:459
  21.7 0.1 collective-permute-done.2.border
  21.8 3.2 %shard_map.78 = (bf16[2,256,256]{2,1,0:T(8,128)(2,1)S(1)}, bf16[2,256,256]{2,1,0:T(8,128)(2,1)S(1)}, bf16[2,256,256]{2,1,0:T(8,128)(2,1)S(1)}) custom-call(s32[1,2]{1,0:T(1,128)S(1)} %copy-done.6, s32[1]{0:T(128)S(6)} %copy.8.live, s16[2,272,256]{2,1,0:T(8,128)(2,1)S(1)} %collective-permute-done.1.direct, ...), custom_call_target="tpu_custom_call" | custom-call | tf_op jit(solution)/shard_map/pallas_call | solution.py:462
  25.0 4.6 %collective-permute-start.5 = (bf16[2,256,256]{2,1,0:T(8,128)(2,1)S(1)}, bf16[2,256,256]{2,1,0:T(8,128)(2,1)S(1)}, u32[]{:S(2)}, u32[]{:S(2)}) collective-permute-start(bf16[2,256,256]{2,1,0:T(8,128)(2,1)S(1)} %get-tuple-element.20), channel_id=1, source_target_pairs={{0,128},{1,129},{2,130},{3,131},{4,132},{5,133},{6,134},{7,135},{8... | collective-permute-start | bytes 786440 | tf_op jit(solution)/shard_map/ppermute | solution.py:444
  29.6 1.1 %collective-permute-done.5.came = bf16[2,256,256]{2,1,0:T(8,128)(2,1)S(1)} collective-permute-done((bf16[2,256,256]{2,1,0:T(8,128)(2,1)S(1)}, bf16[2,256,256]{2,1,0:T(8,128)(2,1)S(1)}, u32[]{:S(2)}, u32[]{:S(2)}) %collective-permute-start.5) | collective-permute-done | bytes 262176 | tf_op jit(solution)/shard_map/ppermute | solution.py:444
  30.7 1.1 %shard_map.80 = f32[2,1,256,512]{3,2,1,0:T(8,128)} custom-call(s32[1,2]{1,0:T(1,128)S(1)} %copy-done.6, s32[1,2]{1,0:T(1,128)S(1)} %collective-permute-done.before, bf16[2,256,256]{2,1,0:T(8,128)(2,1)S(1)} %shard_map.79.stay, bf16[2,256,256]{2,1,0:T(8,128)(2,1)S(1)} %collective-permute-done.5.came), custom_call_target="tpu_custom_call" | custom-call | tf_op jit(solution)/shard_map/pallas_call | solution.py:467
  (2 shorter events, 0.0 us)
Async XLA Ops:
  0.0 2.7 %copy-start.6 = (s32[1,2]{1,0:T(1,128)S(1)}, s32[1,2]{1,0:T(1,128)}, u32[]{:S(2)}) copy-start(s32[1,2]{1,0:T(1,128)} %offsets.11) | copy-start | bytes 28
  0.0 12.2 %collective-permute-start = (s32[1,2]{1,0:T(1,128)}, s32[1,2]{1,0:T(1,128)S(1)}, u32[]{:S(2)}, u32[]{:S(2)}) collective-permute-start(s32[1,2]{1,0:T(1,128)} %offsets.11), channel_id=1, source_target_pairs={{0,1},{1,2},{2,3},{3,4},{4,5},{5,6},{6,7},{7,8},{8,9},{9,10},{10,1... | collective-permute-start | bytes 32 | tf_op jit(solution)/shard_map/ppermute | solution.py:444
  2.7 1.2 %copy-start = (f32[2,1,256,512]{3,2,1,0:T(8,128)S(1)}, f32[2,1,256,512]{3,2,1,0:T(8,128)}, u32[]{:S(2)}) copy-start(f32[2,1,256,512]{3,2,1,0:T(8,128)} %own.7) | copy-start | bytes 3145732
  3.9 8.3 %copy-start.1 = (f32[2,1,256,512]{3,2,1,0:T(8,128)S(1)}, f32[2,1,256,512]{3,2,1,0:T(8,128)}, u32[]{:S(2)}) copy-start(f32[2,1,256,512]{3,2,1,0:T(8,128)} %own.7) | copy-start | bytes 3145732
  3.9 8.3 %copy-start.4 = (f32[1,256,256]{2,1,0:T(8,128)S(1)}, f32[1,256,256]{2,1,0:T(8,128)}, u32[]{:S(2)}) copy-start(f32[1,256,256]{2,1,0:T(8,128)} %measured.3) | copy-start | bytes 786436
  3.9 11.9 %copy-start.5 = (f32[2,256,256]{2,1,0:T(8,128)S(1)}, f32[2,256,256]{2,1,0:T(8,128)}, u32[]{:S(2)}) copy-start(f32[2,256,256]{2,1,0:T(8,128)} %illumination.1) | copy-start | bytes 1572868
  4.2 12.4 %copy-start.2 = (bf16[8,256,256]{2,1,0:T(8,128)(2,1)S(1)}, bf16[8,256,256]{2,1,0:T(8,128)(2,1)}, u32[]{:S(2)}) copy-start(bf16[8,256,256]{2,1,0:T(8,128)(2,1)} %constant.4.clone.prop) | copy-start | bytes 3145732
  4.2 12.5 %collective-permute-start.3 = (s16[2,272,256]{2,1,0:T(8,128)(2,1)S(1)}, s16[2,272,256]{2,1,0:T(8,128)(2,1)S(1)}, u32[]{:S(2)}, u32[]{:S(2)}) collective-permute-start(s16[2,272,256]{2,1,0:T(8,128)(2,1)S(1)} %shard_map.73), channel_id=1, source_target_pairs={{0,128},{1,129},{2,130},{3,131},{4,132},{5,133},{6,134},{7,135},{8... | collective-permute-start | bytes 835592 | tf_op jit(solution)/shard_map/ppermute | solution.py:444
  6.3 10.3 %collective-permute-start.1 = (s16[2,272,256]{2,1,0:T(8,128)(2,1)S(1)}, s16[2,272,256]{2,1,0:T(8,128)(2,1)S(1)}, u32[]{:S(2)}, u32[]{:S(2)}) collective-permute-start(s16[2,272,256]{2,1,0:T(8,128)(2,1)S(1)} %shard_map.73), channel_id=1, source_target_pairs={{0,1},{1,2},{2,3},{3,4},{4,5},{5,6},{6,7},{7,8},{8,9},{9,10},{10,1... | collective-permute-start | bytes 835592 | tf_op jit(solution)/shard_map/ppermute | solution.py:444
  12.5 8.1 %collective-permute-start.4 = (s16[2,272,256]{2,1,0:T(8,128)(2,1)S(1)}, s16[2,272,256]{2,1,0:T(8,128)(2,1)S(1)}, u32[]{:S(2)}, u32[]{:S(2)}) collective-permute-start(s16[2,272,256]{2,1,0:T(8,128)(2,1)S(1)} %get-tuple-element.14), channel_id=1, source_target_pairs={{0,255},{1,128},{2,129},{3,130},{4,131},{5,132},{6,133},{7,134},{8... | collective-permute-start | bytes 835592 | tf_op jit(solution)/shard_map/ppermute | solution.py:444
  14.1 7.7 %collective-permute-start.2 = (s16[2,272,256]{2,1,0:T(8,128)(2,1)S(1)}, s16[2,272,256]{2,1,0:T(8,128)(2,1)S(1)}, u32[]{:S(2)}, u32[]{:S(2)}) collective-permute-start(s16[2,272,256]{2,1,0:T(8,128)(2,1)S(1)} %get-tuple-element.13), channel_id=1, source_target_pairs={{0,1},{1,2},{2,3},{3,4},{4,5},{5,6},{6,7},{7,8},{8,9},{9,10},{10,1... | collective-permute-start | bytes 835592 | tf_op jit(solution)/shard_map/ppermute | solution.py:444
  16.6 4.0 %copy-start.3 = (bf16[6,256,256]{2,1,0:T(8,128)(2,1)S(1)}, bf16[6,256,256]{2,1,0:T(8,128)(2,1)}, u32[]{:S(2)}) copy-start(bf16[6,256,256]{2,1,0:T(8,128)(2,1)} %constant.5.clone.far) | copy-start | bytes 2359300
  25.0 5.7 %collective-permute-start.5 = (bf16[2,256,256]{2,1,0:T(8,128)(2,1)S(1)}, bf16[2,256,256]{2,1,0:T(8,128)(2,1)S(1)}, u32[]{:S(2)}, u32[]{:S(2)}) collective-permute-start(bf16[2,256,256]{2,1,0:T(8,128)(2,1)S(1)} %get-tuple-element.20), channel_id=1, source_target_pairs={{0,128},{1,129},{2,130},{3,131},{4,132},{5,133},{6,134},{7,135},{8... | collective-permute-start | bytes 786440 | tf_op jit(solution)/shard_map/ppermute | solution.py:444
